TPU v7x, 32 devices: a whole 2x2x4 slice. The times are simulated.
32 devices in a mesh: dom: 8 (over z, x), slab: 4 (over y, core).
Axes of the slice: x: 2, y: 2, z: 4, core: 2. Of those that a mesh axis runs over, the one named last changes fastest.
Arguments:
- basis_weights: float32 [4, 4, 12288], P(None, 'slab', 'dom'), may hold values from 0 to 1, as said below
- velocity: float32 [3, 4, 12288], P(None, 'slab', 'dom'), may hold values from -6 to 6
- owner_dom: int32 [4, 12288, 1], P('slab', 'dom'), may hold values from 0 to 7; in each aligned block of 1536 rows (0 to 1535, 1536 to 3071, ..., all dimensions but the last counted through in order) at most 384 rows name the same one
- cell_local: int32 [4, 12288], P('slab', 'dom'), may hold values from 0 to 255
- inverse: float32 [16, 4, 2048], P(None, 'slab', 'dom'), may hold values from -0.2 to 1.5
- connectivity: int32 [4, 4, 2048], P(None, 'slab', 'dom'), may hold values from 0 to 2303, as said below
Outputs:
- coefficients: float32 [12, 4, 2048], P(None, 'slab', 'dom')
- node_values: float32 [3, 4, 2048], P(None, 'slab', 'dom')
Inputs may be any that keep to these rules, and one draw needn't show every extreme that they name: `basis_weights`: the four entries of each particle are positive and sum to one. `owner_dom`: among the rows of one device, no owner is named more than 384 times. `connectivity`: the slab move and dom move are each -1, 0 or 1, and the node they name lies inside the domain.
All inputs are finite; a program needn't handle non-finite values.
Results may differ from a plain program's by a relative error of at most 0.00011.
Values sent between devices are 32-bit elements; how exact they have to be, the bound alone decides.
No kernel may reach another device: no remote copies, remote signals or barrier semaphores. Data moves between devices by JAX's collectives and lax.ppermute only.
A program may use at most 64 MiB of HBM per device.

v0:
```python
import math

import jax
import jax.numpy as jnp
import numpy as np
from jax import lax
from jax.sharding import PartitionSpec as P

NODES_DEV = 256


PAIR_FIRST = np.array([0, 0, 0, 0, 1, 1, 1, 2, 2, 3], dtype=np.int32)
PAIR_SECOND = np.array([0, 1, 2, 3, 1, 2, 3, 2, 3, 3], dtype=np.int32)
GRAM_FROM_PAIR = np.array([0, 1, 2, 3, 1, 4, 5, 6, 2, 5, 7, 8, 3, 6, 8, 9], dtype=np.int32)


def from_behind(array, axis, by):
    devices = lax.axis_size(axis)
    pairs = [(i, i + by) for i in range(devices) if 0 <= i + by < devices]
    return lax.ppermute(array, axis, pairs)


def expand_terms(weights, velocities):
    upper_terms = weights[PAIR_FIRST] * weights[PAIR_SECOND]
    moment_terms = (weights[:, None, :] * velocities[None, :, :]).reshape(12, -1)
    return jnp.concatenate([upper_terms, moment_terms], axis=0)


def onehot_sum(values, segment_ids, segment_count):
    total = segment_ids.shape[0]
    row_count = values.shape[0]
    limit = max(128, 2097152 // segment_count)
    block = math.gcd(total, limit)
    rounds = total // block
    value_blocks = jnp.transpose(values.reshape(row_count, rounds, block), (1, 0, 2))
    id_blocks = segment_ids.reshape(rounds, block)
    columns = jnp.arange(segment_count, dtype=jnp.int32)

    def accumulate(carry, items):
        value_block, id_block = items
        table = (id_block[:, None] == columns[None, :]).astype(jnp.float32)
        return (
            carry
            + jnp.dot(
                value_block,
                table,
                precision=lax.Precision.HIGHEST,
                preferred_element_type=jnp.float32,
            ),
            None,
        )

    start = jnp.zeros((row_count, segment_count), jnp.float32)
    result, unused = lax.scan(accumulate, start, (value_blocks, id_blocks))
    return result


def per_device(basis_weights, velocity, owner_dom, cell_local, inverse, connectivity):
    particles = basis_weights.shape[2]
    cell_count = inverse.shape[2]
    dom_count = lax.axis_size("dom")
    capacity = 2 * particles // dom_count
    slot_count = dom_count * capacity
    destination = owner_dom.reshape(particles)
    sort_order = jnp.argsort(destination, stable=True)
    ranked = destination[sort_order]
    starts = jnp.searchsorted(ranked, jnp.arange(dom_count, dtype=jnp.int32))
    slot_index = ranked * capacity + jnp.arange(particles, dtype=jnp.int32) - starts[ranked]
    weights = basis_weights[:, 0]
    velocities = velocity[:, 0]
    cell_float = cell_local.astype(jnp.float32)
    payload = jnp.concatenate([weights, velocities, cell_float], axis=0)
    empty = jnp.zeros((payload.shape[0], slot_count), jnp.float32)
    outgoing = empty.at[:, slot_index].set(payload[:, sort_order])
    arrived = lax.all_to_all(outgoing, "dom", split_axis=1, concat_axis=1, tiled=True)
    products = expand_terms(arrived[:4], arrived[4:7])
    cell_index = arrived[7].astype(jnp.int32)
    totals = onehot_sum(products, cell_index, cell_count)
    gram_full = totals[:10][GRAM_FROM_PAIR].reshape(4, 4, cell_count)
    moment = totals[10:].reshape(4, 3, cell_count)
    matrix = inverse[:, 0].reshape(4, 4, cell_count)
    first_pass = jnp.sum(matrix[:, :, None, :] * moment[None], axis=1)
    residual_part = moment - jnp.sum(gram_full[:, :, None, :] * first_pass[None], axis=1)
    solved = first_pass + jnp.sum(matrix[:, :, None, :] * residual_part[None], axis=1)
    coefficients = solved.reshape(12, 1, cell_count)
    node_count = NODES_DEV
    bucket = connectivity[:, 0]
    corner_values = jnp.transpose(solved, (1, 0, 2)).reshape(3, 4 * cell_count)
    local_sums = onehot_sum(corner_values, bucket.reshape(-1), 9 * node_count).reshape(
        3, 3, 3, node_count
    )
    from_below = from_behind(local_sums[:, :, 2], "dom", 1)
    from_above = from_behind(local_sums[:, :, 0], "dom", -1)
    merged = local_sums[:, :, 1] + from_below + from_above
    slab_below = from_behind(merged[:, 2], "slab", 1)
    slab_above = from_behind(merged[:, 0], "slab", -1)
    node_values = (merged[:, 1] + slab_below + slab_above).reshape(3, 1, node_count)
    return (coefficients, node_values)


def solution(mesh):
    in_specs = (
        P(None, "slab", "dom"),
        P(None, "slab", "dom"),
        P("slab", "dom", None),
        P("slab", "dom"),
        P(None, "slab", "dom"),
        P(None, "slab", "dom"),
    )
    out_specs = (P(None, "slab", "dom"), P(None, "slab", "dom"))
    return jax.shard_map(
        per_device, mesh=mesh, in_specs=in_specs, out_specs=out_specs, check_vma=False
    )
```

profile of v0, /device:TPU:0, one launch (start us, length us, event | category | flops | bytes accessed | tf_op | source)
XLA Modules:
  0.0 228.4 jit_solution(17716945003019900651)
XLA Ops:
  0.6 0.7 reduce
  1.4 5.0 %sort.17 = (s32[1536]{0:T(1024)}, s32[1536]{0:T(1024)S(1)}) sort(s32[1536]{0:T(1024)S(1)} %reduce, s32[1536]{0:T(1024)S(1)} %iota.17), dimensions={0}, to_apply=%region_0.0 | sort | flops 16896 | bytes 24576 | tf_op jit(solution)/shard_map/jit(argsort)/sort | solution.py:65
  6.4 8.4 %gather_fusion.1 = s32[1536]{0:T(1024)S(1)} fusion(s32[1536]{0:T(1024)S(1)} %reduce, s32[2048]{0:T(1024)S(1)} %pad_clamp_fusion.1), kind=kCustom, calls=%fused_computation.1 | custom fusion | bytes 18432 | tf_op jit(solution)/shard_map/gather | solution.py:66
  14.9 7.6 %while.46 = (s32[]{:T(128)}, u32[8]{0:T(128)S(1)}, u32[8]{0:T(128)S(1)}, s32[1536]{0:T(1024)S(1)}, s32[]{:T(128)}, /*index=5*/s32[]{:T(128)}, s32[]{}) while((s32[]{:T(128)}, u32[8]{0:T(128)S(1)}, u32[8]{0:T(128)S(1)}, s32[1536]{0:T(1024)S(1)}, s32[]{:T(128)}, /*index=5*/s32[]{:T(128)}, s32[]{}) %tuple.91), condition=%wide.region_2.3_spmd.clone, body=%wide.region_1.2_spmd.clone.sunk | while | flops 1132 | bytes 4580 | solution.py:67
  14.9 0.6 gather_fusion
  15.6 0.6 gather_fusion
  16.3 0.6 gather_fusion
  17.0 0.6 gather_fusion
  17.7 0.6 gather_fusion
  18.4 0.6 gather_fusion
  19.1 0.6 gather_fusion
  19.8 0.6 gather_fusion
  20.5 0.6 gather_fusion
  21.2 0.6 gather_fusion
  21.9 0.6 gather_fusion
  22.5 0.7 fusion.28
  23.2 4.4 %fusion.21 = s32[1536]{0:T(1024)S(1)} fusion(s32[]{:T(128)} %bitcast.1, s32[]{:T(128)} %bitcast.2, s32[]{:T(128)} %bitcast.3, s32[]{:T(128)} %bitcast.4, s32[]{:T(128)} %bitcast.5, s32[]{:T(128)} %bitcast.7, s32[]{:T(128)} %bitcast.6, s32[1536]{0:T(1024)S(1)} %get-tuple-element.381), kind=kLoop, calls=%fused_computation.60 | loop fusion | flops 23040 | bytes 12316 | tf_op jit(solution)/shard_map/gather | solution.py:68
  27.7 0.7 broadcast_select_fusion.2
  28.8 10.0 %scatter_custom_fusion = f32[8,3072]{0,1:T(8,128)S(1)} fusion(s32[1536]{0:T(1024)S(1)} %fusion.22, f32[8,1536]{0,1:T(8,128)S(1)} %copy.55, s32[2048]{0:T(1024)S(1)} %pad_clamp_fusion.1, f32[]{:T(128)} %constant.69.clone.1), kind=kCustom, calls=%fused_computation.31 | custom fusion | bytes 98308 | tf_op jit(solution)/shard_map/scatter | solution.py:74
  38.8 1.1 copy.56
  39.9 7.3 %all-to-all-start = ((f32[8,8,384]{2,0,1:T(8,128)}), f32[8,8,384]{2,0,1:T(8,128)S(1)}, u32[]{:S(2)}, u32[]{:S(2)}) async-start(f32[8,8,384]{2,0,1:T(8,128)} %copy.56), calls=%async_computation | async-start | bytes 196608 | tf_op jit(solution)/shard_map/all_to_all | solution.py:75
  47.5 6.7 %all-to-all-done = f32[8,8,384]{2,0,1:T(8,128)S(1)} async-done(((f32[8,8,384]{2,0,1:T(8,128)}), f32[8,8,384]{2,0,1:T(8,128)S(1)}, u32[]{:S(2)}, u32[]{:S(2)}) %all-to-all-start) | async-done | bytes 98336 | tf_op jit(solution)/shard_map/all_to_all | solution.py:75
  56.0 2.0 while.47
  58.8 0.8 reshape_reshape.3
  59.6 3.2 %copy.62 = f32[512,3,2]{1,2,0:T(2,128)S(1)} copy(f32[512,3,2]{2,0,1:T(8,128)S(1)} %bitcast.70) | data formatting | bytes 24576
  62.8 150.9 %while.48 = (s32[]{:T(128)}, f32[3,2304]{1,0:T(4,128)S(1)}, f32[512,3,2]{1,2,0:T(2,128)S(1)}, s32[512,2]{1,0:T(8,128)S(1)}, s32[]{:T(128)}, /*index=5*/s32[]{:T(128)}) while((s32[]{:T(128)}, f32[3,2304]{1,0:T(4,128)S(1)}, f32[512,3,2]{1,2,0:T(2,128)S(1)}, s32[512,2]{1,0:T(8,128)S(1)}, s32[]{:T(128)}, /*index=5*/s32[]{:T(128)}) %tuple.97), condition=%wide.region_10.11_spmd.clone, body=%wide.region_9.10_spmd.clone.sunk | while | flops 184323 | bytes 66151 | solution.py:54
  213.8 2.2 collective-permute-start
  216.0 1.3 collective-permute-start.1
  217.4 4.2 %collective-permute-done.1 = f32[3,3,256]{2,1,0:T(4,128)S(1)} collective-permute-done((f32[3,3,256]{2,1,0:T(4,128)S(1)}, f32[3,3,256]{2,1,0:T(4,128)S(1)}, u32[]{:S(2)}, u32[]{:S(2)}) %collective-permute-start.1) | collective-permute-done | bytes 9248 | tf_op jit(solution)/shard_map/ppermute | solution.py:20
  221.6 1.3 collective-permute-start.2
  223.0 1.3 collective-permute-start.3
  224.9 2.9 %collective-permute-done.3 = f32[3,256]{1,0:T(4,128)S(1)} collective-permute-done((f32[3,256]{1,0:T(4,128)S(1)}, f32[3,256]{1,0:T(4,128)S(1)}, u32[]{:S(2)}, u32[]{:S(2)}) %collective-permute-start.3) | collective-permute-done | bytes 3104 | tf_op jit(solution)/shard_map/ppermute | solution.py:20
  (1142 shorter events, 146.0 us)
Async XLA Ops:
  14.8 13.5 %copy-start.1 = (f32[3,1,1536]{2,1,0:T(1,128)S(1)}, f32[3,1,1536]{2,1,0:T(1,128)}, u32[]{:S(2)}) copy-start(f32[3,1,1536]{2,1,0:T(1,128)} %param.19) | copy-start | bytes 55300
  14.8 13.6 %copy-start = (f32[4,1,1536]{2,1,0:T(1,128)S(1)}, f32[4,1,1536]{2,1,0:T(1,128)}, u32[]{:S(2)}) copy-start(f32[4,1,1536]{2,1,0:T(1,128)} %param.18) | copy-start | bytes 73732
  14.8 13.6 %copy-start.3 = (s32[1,1536]{1,0:T(1,128)S(1)}, s32[1,1536]{1,0:T(1,128)}, u32[]{:S(2)}) copy-start(s32[1,1536]{1,0:T(1,128)} %param.21) | copy-start | bytes 18436
  28.7 18.4 %copy-start.7 = (s32[10]{0:T(128)S(1)}, s32[10]{0:T(128)}, u32[]{:S(2)}) copy-start(s32[10]{0:T(128)} %constant.99) | copy-start | bytes 124
  28.8 18.4 %copy-start.2 = (f32[16,1,256]{2,1,0:T(1,128)S(1)}, f32[16,1,256]{2,1,0:T(1,128)}, u32[]{:S(2)}) copy-start(f32[16,1,256]{2,1,0:T(1,128)} %param.22) | copy-start | bytes 49156
  28.8 18.5 %copy-start.4 = (s32[4,1,256]{2,1,0:T(1,128)S(1)}, s32[4,1,256]{2,1,0:T(1,128)}, u32[]{:S(2)}) copy-start(s32[4,1,256]{2,1,0:T(1,128)} %param.23) | copy-start | bytes 12292
  28.8 18.7 %copy-start.6 = (s32[10]{0:T(128)S(1)}, s32[10]{0:T(128)}, u32[]{:S(2)}) copy-start(s32[10]{0:T(128)} %constant.100) | copy-start | bytes 124
  28.8 18.7 %copy-start.5 = (s32[16]{0:T(128)S(1)}, s32[16]{0:T(128)}, u32[]{:S(2)}) copy-start(s32[16]{0:T(128)} %constant.101) | copy-start | bytes 196
  39.9 14.4 %all-to-all-start = ((f32[8,8,384]{2,0,1:T(8,128)}), f32[8,8,384]{2,0,1:T(8,128)S(1)}, u32[]{:S(2)}, u32[]{:S(2)}) async-start(f32[8,8,384]{2,0,1:T(8,128)} %copy.56), calls=%async_computation | async-start | bytes 196608 | tf_op jit(solution)/shard_map/all_to_all | solution.py:75
  213.8 3.6 %collective-permute-start = (f32[3,3,256]{2,1,0:T(4,128)S(1)}, f32[3,3,256]{2,1,0:T(4,128)S(1)}, u32[]{:S(2)}, u32[]{:S(2)}) collective-permute-start(f32[3,3,256]{2,1,0:T(4,128)S(1)} %bitcast.76), channel_id=1, source_target_pairs={{0,4},{4,8},{8,12},{12,16},{16,20},{20,24},{24,28},{1,5},{5,9},{9,... | collective-permute-start | bytes 27656 | tf_op jit(solution)/shard_map/ppermute | solution.py:20
  216.0 5.6 %collective-permute-start.1 = (f32[3,3,256]{2,1,0:T(4,128)S(1)}, f32[3,3,256]{2,1,0:T(4,128)S(1)}, u32[]{:S(2)}, u32[]{:S(2)}) collective-permute-start(f32[3,3,256]{2,1,0:T(4,128)S(1)} %bitcast.77), channel_id=1, source_target_pairs={{4,0},{8,4},{12,8},{16,12},{20,16},{24,20},{28,24},{5,1},{9,5},{13... | collective-permute-start | bytes 27656 | tf_op jit(solution)/shard_map/ppermute | solution.py:20
  221.6 3.2 %collective-permute-start.2 = (f32[3,256]{1,0:T(4,128)S(1)}, f32[3,256]{1,0:T(4,128)S(1)}, u32[]{:S(2)}, u32[]{:S(2)}) collective-permute-start(f32[3,256]{1,0:T(4,128)S(1)} %bitcast.78), channel_id=1, source_target_pairs={{0,1},{1,2},{2,3},{4,5},{5,6},{6,7},{8,9},{9,10},{10,11},{12,13},{... | collective-permute-start | bytes 9224 | tf_op jit(solution)/shard_map/ppermute | solution.py:20
  223.0 4.8 %collective-permute-start.3 = (f32[3,256]{1,0:T(4,128)S(1)}, f32[3,256]{1,0:T(4,128)S(1)}, u32[]{:S(2)}, u32[]{:S(2)}) collective-permute-start(f32[3,256]{1,0:T(4,128)S(1)} %bitcast.79), channel_id=1, source_target_pairs={{1,0},{2,1},{3,2},{5,4},{6,5},{7,6},{9,8},{10,9},{11,10},{13,12},{... | collective-permute-start | bytes 9224 | tf_op jit(solution)/shard_map/ppermute | solution.py:20
where the time goes:
time: 231 us; the launch traced here: 228 us
  matrix products  136 us (59%)
  local copies, waits for them, and re-layouts  40.2 us (17%)
  waiting for transfers between devices  13.9 us (6%)
  starting transfers between devices  13.3 us (6%)
  loops' own time  12 us (5%)
  other arithmetic  11.7 us (5%)
    dot_general x515, matrix products, accumulate(): jnp.dot(value_block, table, precision=lax.Precision.HIGHEST, preferred_el...  136 us
    another operation x2, loops' own time, onehot_sum(): result, unused = lax.scan(accumulate, start, (value_blocks, id_blocks))  11.7 us
    scatter x1, local copies, waits for them, and re-layouts, per_device(): outgoing = empty.at[:, slot_index].set(payload[:, sort_order])  10 us
    gather x1, local copies, waits for them, and re-layouts, per_device(): ranked = destination[sort_order]  8.39 us
    all_to_all x1, starting transfers between devices, per_device(): lax.all_to_all(outgoing, 'dom', split_axis=1, concat_axis=1, tiled=True)  7.25 us
    ppermute x4, waiting for transfers between devices, from_behind(): return lax.ppermute(array, axis, pairs)  7.18 us
    gather x11, local copies, waits for them, and re-layouts, per_device(): starts = jnp.searchsorted(ranked, jnp.arange(dom_count, dtype=jnp.int32))  6.99 us
    all_to_all x1, waiting for transfers between devices, per_device(): lax.all_to_all(outgoing, 'dom', split_axis=1, concat_axis=1, tiled=True)  6.73 us
  transfers between devices with their start and end apart: 5, of which 4 were waited for; matrix products, arithmetic and copies ran while one was open for 0% of the time, Pallas kernels for 0%

commit v1 on v0

v1 whole, which is shorter than its diff:
```python
import jax
import jax.numpy as jnp
from jax import lax
from jax.experimental import pallas as pl
from jax.experimental.pallas import tpu as pltpu
from jax.sharding import PartitionSpec as P

DOM_BLOCK = 8
TERMS = 24
NT = (((1,), (1,)), ((), ()))


def split_rows(values):
    high = values.astype(jnp.bfloat16)
    low = (values - high.astype(jnp.float32)).astype(jnp.bfloat16)
    return high, low


def one_hot_rows(index_row, count):
    rows = lax.broadcasted_iota(jnp.int32, (count, index_row.shape[1]), 0)
    return jnp.where(rows == index_row, 1.0, 0.0).astype(jnp.bfloat16)


def partial_sums_kernel(weights_ref, velocity_ref, owner_ref, cell_ref, sums_ref):
    cell_count = sums_ref.shape[2]
    first_dom = pl.program_id(0) * DOM_BLOCK
    w = weights_ref[:, 0, :]
    v = velocity_ref[:, 0, :]
    particles = w.shape[1]
    wide = (4, particles)
    turned = jnp.concatenate([w[1:], w[:1]], axis=0)
    across = jnp.concatenate([w[2:], w[:2]], axis=0)
    terms = jnp.concatenate(
        [
            w * w,
            w * turned,
            w * across,
            w * jnp.broadcast_to(v[0:1], wide),
            w * jnp.broadcast_to(v[1:2], wide),
            w * jnp.broadcast_to(v[2:3], wide),
        ],
        axis=0,
    )
    high, low = split_rows(terms)
    both = jnp.concatenate([high, low], axis=0)
    owner = owner_ref[...]
    picked = []
    for d in range(DOM_BLOCK):
        named = jnp.where(owner == first_dom + d, 1.0, 0.0).astype(jnp.bfloat16)
        picked.append(both * named)
    left = jnp.concatenate(picked, axis=0)
    right = one_hot_rows(cell_ref[...], cell_count)
    sums = lax.dot_general(left, right, NT, preferred_element_type=jnp.float32)
    for d in range(DOM_BLOCK):
        at = 2 * TERMS * d
        sums_ref[d] = sums[at : at + TERMS] + sums[at + TERMS : at + 2 * TERMS]


def partial_sums(basis_weights, velocity, owner, cell_local, dom_count, cell_count):
    particles = cell_local.shape[1]
    full = lambda shape: pl.BlockSpec(shape, lambda i: (0,) * len(shape))
    return pl.pallas_call(
        partial_sums_kernel,
        grid=(dom_count // DOM_BLOCK,),
        in_specs=[
            full((4, 1, particles)),
            full((3, 1, particles)),
            full((1, particles)),
            full((1, particles)),
        ],
        out_specs=pl.BlockSpec((DOM_BLOCK, TERMS, cell_count), lambda i: (i, 0, 0)),
        out_shape=jax.ShapeDtypeStruct((dom_count, TERMS, cell_count), jnp.float32),
        compiler_params=pltpu.CompilerParams(vmem_limit_bytes=48 * 1024 * 1024),
        name="partial_sums",
    )(basis_weights, velocity, owner, cell_local)


def solve_kernel(arrived_ref, inverse_ref, connectivity_ref, coefficients_ref, nodes_ref):
    cells = arrived_ref.shape[2]
    nodes = nodes_ref.shape[2]
    total = arrived_ref[0]
    for d in range(1, arrived_ref.shape[0]):
        total = total + arrived_ref[d]

    def gram(i, j):
        if i == j:
            row = i
        elif (j - i) % 4 == 1:
            row = 4 + i
        elif (i - j) % 4 == 1:
            row = 4 + j
        else:
            row = 8 + i
        return total[row : row + 1]

    wide = (4, cells)
    inverse_columns = [
        jnp.concatenate([inverse_ref[4 * i + j] for i in range(4)], axis=0) for j in range(4)
    ]
    gram_columns = [jnp.concatenate([gram(i, j) for i in range(4)], axis=0) for j in range(4)]
    solved = []
    for a in range(3):
        moment = total[12 + 4 * a : 16 + 4 * a]

        def apply(columns, vector):
            parts = [columns[j] * jnp.broadcast_to(vector[j : j + 1], wide) for j in range(4)]
            return (parts[0] + parts[1]) + (parts[2] + parts[3])

        first = apply(inverse_columns, moment)
        residual = moment - apply(gram_columns, first)
        solved.append(first + apply(inverse_columns, residual))
    for i in range(4):
        for a in range(3):
            coefficients_ref[3 * i + a] = solved[a][i : i + 1]
    left, right = [], []
    for k in range(4):
        values = jnp.concatenate(
            [solved[a][k : k + 1] for a in range(3)] + [jnp.zeros((1, cells), jnp.float32)], axis=0
        )
        values = jnp.concatenate([values, values], axis=0)
        entry = connectivity_ref[k]
        move = entry // nodes
        node = entry - move * nodes
        columns = []
        for m in range(0, 10, 2):
            rows = lax.broadcasted_iota(jnp.int32, (8, cells), 0) // 4 + m
            columns.append(jnp.where(rows == move, values, 0.0))
        left.append(jnp.concatenate(columns, axis=0))
        right.append(one_hot_rows(node, nodes))
    left = jnp.concatenate(left, axis=1)
    right = jnp.concatenate(right, axis=1)
    high, low = split_rows(left)
    both = jnp.concatenate([high, low], axis=0)
    sums = lax.dot_general(both, right, NT, preferred_element_type=jnp.float32)
    sums = sums[:40] + sums[40:]
    for m in range(9):
        nodes_ref[m] = sums[4 * m : 4 * m + 3]


def solve(arrived, inverse, connectivity, node_count):
    cells = arrived.shape[2]
    return pl.pallas_call(
        solve_kernel,
        out_shape=(
            jax.ShapeDtypeStruct((12, 1, cells), jnp.float32),
            jax.ShapeDtypeStruct((9, 3, node_count), jnp.float32),
        ),
        compiler_params=pltpu.CompilerParams(vmem_limit_bytes=48 * 1024 * 1024),
        name="solve",
    )(arrived, inverse, connectivity)


def shifted(array, axis, by):
    devices = lax.axis_size(axis)
    pairs = [(i, i + by) for i in range(devices) if 0 <= i + by < devices]
    return lax.ppermute(array, axis, pairs)


def per_device(basis_weights, velocity, owner_dom, cell_local, inverse, connectivity):
    particles = cell_local.shape[1]
    cells = inverse.shape[2]
    nodes = 256
    doms = lax.axis_size("dom")
    owner = owner_dom.reshape(1, particles)
    sums = partial_sums(basis_weights, velocity, owner, cell_local, doms, cells)
    arrived = lax.all_to_all(sums, "dom", split_axis=0, concat_axis=0, tiled=True)
    coefficients, local = solve(arrived, inverse, connectivity, nodes)
    local = local.reshape(3, 3, 3, nodes)
    merged = local[:, 1] + shifted(local[:, 2], "dom", 1) + shifted(local[:, 0], "dom", -1)
    total = merged[1] + shifted(merged[2], "slab", 1) + shifted(merged[0], "slab", -1)
    return coefficients, total.reshape(3, 1, nodes)


def solution(mesh):
    in_specs = (
        P(None, "slab", "dom"),
        P(None, "slab", "dom"),
        P("slab", "dom", None),
        P("slab", "dom"),
        P(None, "slab", "dom"),
        P(None, "slab", "dom"),
    )
    out_specs = (P(None, "slab", "dom"), P(None, "slab", "dom"))
    return jax.shard_map(
        per_device, mesh=mesh, in_specs=in_specs, out_specs=out_specs, check_vma=False
    )
```

time: 231 us -> 37.4 us (0.16)
  the two profiles are of different devices: /device:TPU:0 before, /device:TPU:1 now
where the time goes in v1:
time: 37.4 us; the launch traced here: 37 us
  blocking collectives  12.8 us (34%)
  starting transfers between devices  12.6 us (34%)
  waiting for transfers between devices  6.12 us (16%)
  local copies, waits for them, and re-layouts  3.44 us (9%)
  Pallas kernels  1.24 us (3%)
  between operations  0.72 us (2%)
    all_to_all x1, blocking collectives, per_device(): lax.all_to_all(sums, 'dom', split_axis=0, concat_axis=0, tiled=True)  12.8 us
    ppermute x4, starting transfers between devices, shifted(): return lax.ppermute(array, axis, pairs)  12.6 us
    ppermute x4, waiting for transfers between devices, shifted(): return lax.ppermute(array, axis, pairs)  6.12 us
    unnamed x12, local copies, waits for them, and re-layouts  2.85 us
  transfers between devices with their start and end apart: 4, of which 2 were waited for; matrix products, arithmetic and copies ran while one was open for 0% of the time, Pallas kernels for 0%

profile of v1, /device:TPU:1, one launch (start us, length us, event | category | flops | bytes accessed | tf_op | source)
XLA Modules:
  0.0 37.0 jit_solution(17673061983409261023)
XLA Ops:
  0.6 0.0 copy-start
  0.6 0.7 %copy-done = f32[4,1,1536]{2,1,0:T(1,128)S(1)} copy-done((f32[4,1,1536]{2,1,0:T(1,128)S(1)}, f32[4,1,1536]{2,1,0:T(1,128)}, u32[]{:S(2)}) %copy-start) | copy-done | bytes 24600
  1.4 0.0 copy-start.1
  1.4 0.7 %copy-done.1 = f32[3,1,1536]{2,1,0:T(1,128)S(1)} copy-done((f32[3,1,1536]{2,1,0:T(1,128)S(1)}, f32[3,1,1536]{2,1,0:T(1,128)}, u32[]{:S(2)}) %copy-start.1) | copy-done | bytes 18456
  2.1 0.0 copy-start.3
  2.1 0.7 %copy-done.3 = s32[1,1536,1]{1,2,0:T(1,128)S(1)} copy-done((s32[1,1536,1]{1,2,0:T(1,128)S(1)}, s32[1,1536,1]{1,2,0:T(1,128)}, u32[]{:S(2)}) %copy-start.3) | copy-done | bytes 6168
  2.8 0.0 copy-start.4
  2.8 0.7 %copy-done.4 = s32[1,1536]{1,0:T(1,128)S(1)} copy-done((s32[1,1536]{1,0:T(1,128)S(1)}, s32[1,1536]{1,0:T(1,128)}, u32[]{:S(2)}) %copy-start.4) | copy-done | bytes 6168
  3.5 0.5 %partial_sums.1 = f32[8,24,256]{2,1,0:T(8,128)S(1)} custom-call(f32[4,1,1536]{2,1,0:T(1,128)S(1)} %copy-done, f32[3,1,1536]{2,1,0:T(1,128)S(1)} %copy-done.1, s32[1,1536]{1,0:T(1,128)S(1)} %bitcast.30, s32[1,1536]{1,0:T(1,128)S(1)} %copy-done.4), custom_call_target="tpu_custom_call" | custom-call | tf_op jit(solution)/shard_map/partial_sums/pallas_call | solution.py:62
  4.0 0.0 copy-start.2
  4.0 0.0 copy-start.5
  4.0 12.8 %all_to_all.5.arrived_ref = f32[8,24,256]{2,1,0:T(8,128)S(1)} all-to-all(f32[8,24,256]{2,1,0:T(8,128)S(1)} %partial_sums.1), channel_id=1, replica_groups=mesh['dom'=8,'slab'=4] {'dom'}, dimensions={0} | all-to-all | bytes 393216 | tf_op jit(solution)/shard_map/all_to_all | solution.py:166
  16.8 0.0 copy-done.2
  16.8 0.0 copy-done.5
  16.8 0.7 %solve.1 = (f32[12,1,256]{2,1,0:T(1,128)}, f32[9,3,256]{2,1,0:T(4,128)S(1)}) custom-call(f32[8,24,256]{2,1,0:T(8,128)S(1)} %all_to_all.5.arrived_ref, f32[16,1,256]{2,1,0:T(1,128)S(1)} %copy-done.2, s32[4,1,256]{2,1,0:T(1,128)S(1)} %copy-done.5), custom_call_target="tpu_custom_call" | custom-call | tf_op jit(solution)/shard_map/solve/pallas_call | solution.py:142
  17.6 1.6 %collective-permute-start = (f32[3,3,256]{2,1,0:T(4,128)S(1)}, f32[3,3,256]{2,1,0:T(4,128)S(1)}, u32[]{:S(2)}, u32[]{:S(2)}) collective-permute-start(f32[3,3,256]{2,1,0:T(4,128)S(1)} %get-tuple-element.6), channel_id=1, source_target_pairs={{0,4},{4,8},{8,12},{12,16},{16,20},{20,24},{24,28},{1,5},{5,9},{9,... | collective-permute-start | bytes 27656 | tf_op jit(solution)/shard_map/ppermute | solution.py:156
  19.2 1.3 %collective-permute-start.1 = (f32[3,3,256]{2,1,0:T(4,128)S(1)}, f32[3,3,256]{2,1,0:T(4,128)S(1)}, u32[]{:S(2)}, u32[]{:S(2)}) collective-permute-start(f32[3,3,256]{2,1,0:T(4,128)S(1)} %get-tuple-element.7), channel_id=1, source_target_pairs={{4,0},{8,4},{12,8},{16,12},{20,16},{24,20},{28,24},{5,1},{9,5},{13... | collective-permute-start | bytes 27656 | tf_op jit(solution)/shard_map/ppermute | solution.py:156
  20.5 0.0 collective-permute-done
  20.5 3.1 %collective-permute-done.1 = f32[3,3,256]{2,1,0:T(4,128)S(1)} collective-permute-done((f32[3,3,256]{2,1,0:T(4,128)S(1)}, f32[3,3,256]{2,1,0:T(4,128)S(1)}, u32[]{:S(2)}, u32[]{:S(2)}) %collective-permute-start.1) | collective-permute-done | bytes 9248 | tf_op jit(solution)/shard_map/ppermute | solution.py:156
  23.7 7.8 %collective-permute-start.2 = (f32[3,256]{1,0:T(4,128)S(1)}, f32[3,256]{1,0:T(4,128)S(1)}, u32[]{:S(2)}, u32[]{:S(2)}) collective-permute-start(f32[3,256]{1,0:T(4,128)S(1)} %get-tuple-element.8), channel_id=1, source_target_pairs={{0,1},{1,2},{2,3},{4,5},{5,6},{6,7},{8,9},{9,10},{10,11},{12,13},{... | collective-permute-start | bytes 9224 | tf_op jit(solution)/shard_map/ppermute | solution.py:156
  31.4 1.9 %collective-permute-start.3 = (f32[3,256]{1,0:T(4,128)S(1)}, f32[3,256]{1,0:T(4,128)S(1)}, u32[]{:S(2)}, u32[]{:S(2)}) collective-permute-start(f32[3,256]{1,0:T(4,128)S(1)} %get-tuple-element.9), channel_id=1, source_target_pairs={{1,0},{2,1},{3,2},{5,4},{6,5},{7,6},{9,8},{10,9},{11,10},{13,12},{... | collective-permute-start | bytes 9224 | tf_op jit(solution)/shard_map/ppermute | solution.py:156
  33.4 0.0 collective-permute-done.2
  33.4 3.0 %collective-permute-done.3 = f32[3,256]{1,0:T(4,128)S(1)} collective-permute-done((f32[3,256]{1,0:T(4,128)S(1)}, f32[3,256]{1,0:T(4,128)S(1)}, u32[]{:S(2)}, u32[]{:S(2)}) %collective-permute-start.3) | collective-permute-done | bytes 3104 | tf_op jit(solution)/shard_map/ppermute | solution.py:156
  36.4 0.6 %reshape.15 = f32[3,1,256]{2,1,0:T(1,128)} reshape(f32[3,256]{1,0:T(4,128)S(1)} %fusion.3) | data formatting | bytes 6144 | tf_op jit(solution)/shard_map/reshape | solution.py:171
  (4 shorter events, 0.0 us)
Async XLA Ops:
  0.6 0.7 %copy-start = (f32[4,1,1536]{2,1,0:T(1,128)S(1)}, f32[4,1,1536]{2,1,0:T(1,128)}, u32[]{:S(2)}) copy-start(f32[4,1,1536]{2,1,0:T(1,128)} %weights_ref.1) | copy-start | bytes 73732
  1.4 0.7 %copy-start.1 = (f32[3,1,1536]{2,1,0:T(1,128)S(1)}, f32[3,1,1536]{2,1,0:T(1,128)}, u32[]{:S(2)}) copy-start(f32[3,1,1536]{2,1,0:T(1,128)} %velocity_ref.1) | copy-start | bytes 55300
  2.1 0.7 %copy-start.3 = (s32[1,1536,1]{1,2,0:T(1,128)S(1)}, s32[1,1536,1]{1,2,0:T(1,128)}, u32[]{:S(2)}) copy-start(s32[1,1536,1]{1,2,0:T(1,128)} %param.8) | copy-start | bytes 18436
  2.8 0.7 %copy-start.4 = (s32[1,1536]{1,0:T(1,128)S(1)}, s32[1,1536]{1,0:T(1,128)}, u32[]{:S(2)}) copy-start(s32[1,1536]{1,0:T(1,128)} %cell_ref.1) | copy-start | bytes 18436
  4.0 12.8 %copy-start.2 = (f32[16,1,256]{2,1,0:T(1,128)S(1)}, f32[16,1,256]{2,1,0:T(1,128)}, u32[]{:S(2)}) copy-start(f32[16,1,256]{2,1,0:T(1,128)} %inverse_ref.1) | copy-start | bytes 49156
  4.0 12.8 %copy-start.5 = (s32[4,1,256]{2,1,0:T(1,128)S(1)}, s32[4,1,256]{2,1,0:T(1,128)}, u32[]{:S(2)}) copy-start(s32[4,1,256]{2,1,0:T(1,128)} %connectivity_ref.1) | copy-start | bytes 12292
  17.6 2.9 %collective-permute-start = (f32[3,3,256]{2,1,0:T(4,128)S(1)}, f32[3,3,256]{2,1,0:T(4,128)S(1)}, u32[]{:S(2)}, u32[]{:S(2)}) collective-permute-start(f32[3,3,256]{2,1,0:T(4,128)S(1)} %get-tuple-element.6), channel_id=1, source_target_pairs={{0,4},{4,8},{8,12},{12,16},{16,20},{20,24},{24,28},{1,5},{5,9},{9,... | collective-permute-start | bytes 27656 | tf_op jit(solution)/shard_map/ppermute | solution.py:156
  19.2 4.4 %collective-permute-start.1 = (f32[3,3,256]{2,1,0:T(4,128)S(1)}, f32[3,3,256]{2,1,0:T(4,128)S(1)}, u32[]{:S(2)}, u32[]{:S(2)}) collective-permute-start(f32[3,3,256]{2,1,0:T(4,128)S(1)} %get-tuple-element.7), channel_id=1, source_target_pairs={{4,0},{8,4},{12,8},{16,12},{20,16},{24,20},{28,24},{5,1},{9,5},{13... | collective-permute-start | bytes 27656 | tf_op jit(solution)/shard_map/ppermute | solution.py:156
  23.7 9.7 %collective-permute-start.2 = (f32[3,256]{1,0:T(4,128)S(1)}, f32[3,256]{1,0:T(4,128)S(1)}, u32[]{:S(2)}, u32[]{:S(2)}) collective-permute-start(f32[3,256]{1,0:T(4,128)S(1)} %get-tuple-element.8), channel_id=1, source_target_pairs={{0,1},{1,2},{2,3},{4,5},{5,6},{6,7},{8,9},{9,10},{10,11},{12,13},{... | collective-permute-start | bytes 9224 | tf_op jit(solution)/shard_map/ppermute | solution.py:156
  31.4 4.9 %collective-permute-start.3 = (f32[3,256]{1,0:T(4,128)S(1)}, f32[3,256]{1,0:T(4,128)S(1)}, u32[]{:S(2)}, u32[]{:S(2)}) collective-permute-start(f32[3,256]{1,0:T(4,128)S(1)} %get-tuple-element.9), channel_id=1, source_target_pairs={{1,0},{2,1},{3,2},{5,4},{6,5},{7,6},{9,8},{10,9},{11,10},{13,12},{... | collective-permute-start | bytes 9224 | tf_op jit(solution)/shard_map/ppermute | solution.py:156

commit v2 on v1

--- a/solution.py
+++ b/solution.py
@@ -21,7 +21,28 @@
     return jnp.where(rows == index_row, 1.0, 0.0).astype(jnp.bfloat16)
 
 
-def partial_sums_kernel(weights_ref, velocity_ref, owner_ref, cell_ref, sums_ref):
+def partial_sums_kernel(
+    weights_hbm, velocity_hbm, owner_hbm, cell_hbm, sums_ref,
+    weights_ref, velocity_ref, owner_ref, cell_ref, arrivals,
+):
+    pairs = (
+        (weights_hbm, weights_ref),
+        (velocity_hbm, velocity_ref),
+        (owner_hbm, owner_ref),
+        (cell_hbm, cell_ref),
+    )
+
+    @pl.when(pl.program_id(0) == 0)
+    def _():
+        copies = [
+            pltpu.make_async_copy(source, target, arrivals.at[i])
+            for i, (source, target) in enumerate(pairs)
+        ]
+        for copy in copies:
+            copy.start()
+        for copy in copies:
+            copy.wait()
+
     cell_count = sums_ref.shape[2]
     first_dom = pl.program_id(0) * DOM_BLOCK
     w = weights_ref[:, 0, :]
@@ -58,26 +79,35 @@
 
 def partial_sums(basis_weights, velocity, owner, cell_local, dom_count, cell_count):
     particles = cell_local.shape[1]
-    full = lambda shape: pl.BlockSpec(shape, lambda i: (0,) * len(shape))
     return pl.pallas_call(
         partial_sums_kernel,
         grid=(dom_count // DOM_BLOCK,),
-        in_specs=[
-            full((4, 1, particles)),
-            full((3, 1, particles)),
-            full((1, particles)),
-            full((1, particles)),
-        ],
+        in_specs=[pl.BlockSpec(memory_space=pltpu.HBM)] * 4,
         out_specs=pl.BlockSpec((DOM_BLOCK, TERMS, cell_count), lambda i: (i, 0, 0)),
         out_shape=jax.ShapeDtypeStruct((dom_count, TERMS, cell_count), jnp.float32),
+        scratch_shapes=[
+            pltpu.VMEM((4, 1, particles), jnp.float32),
+            pltpu.VMEM((3, 1, particles), jnp.float32),
+            pltpu.VMEM((1, particles), jnp.int32),
+            pltpu.VMEM((1, particles), jnp.int32),
+            pltpu.SemaphoreType.DMA((4,)),
+        ],
         compiler_params=pltpu.CompilerParams(vmem_limit_bytes=48 * 1024 * 1024),
         name="partial_sums",
-    )(basis_weights, velocity, owner, cell_local)
-
-
-def solve_kernel(arrived_ref, inverse_ref, connectivity_ref, coefficients_ref, nodes_ref):
+    )(*(pltpu.with_memory_space_constraint(a, pltpu.HBM) for a in (basis_weights, velocity, owner, cell_local)))
+
+
+def solve_kernel(
+    arrived_ref, inverse_ref, connectivity_ref,
+    coefficients_ref, dom_far_ref, dom_near_ref, own_ref,
+):
     cells = arrived_ref.shape[2]
-    nodes = nodes_ref.shape[2]
+    nodes = own_ref.shape[2]
+    dom_odd = lax.rem(lax.axis_index("dom"), 2)
+    slab_odd = lax.rem(lax.axis_index("slab"), 2)
+    dom_moves = (2 * dom_odd, 2 - 2 * dom_odd, 1)
+    slab_moves = (2 * slab_odd, 2 - 2 * slab_odd, 1)
+    wanted = [3 * slab_move + dom_move for dom_move in dom_moves for slab_move in slab_moves]
     total = arrived_ref[0]
     for d in range(1, arrived_ref.shape[0]):
         total = total + arrived_ref[d]
@@ -122,8 +152,9 @@
         move = entry // nodes
         node = entry - move * nodes
         columns = []
+        upper = lax.broadcasted_iota(jnp.int32, (8, cells), 0) < 4
         for m in range(0, 10, 2):
-            rows = lax.broadcasted_iota(jnp.int32, (8, cells), 0) // 4 + m
+            rows = jnp.where(upper, wanted[m], wanted[m + 1] if m < 8 else -1)
             columns.append(jnp.where(rows == move, values, 0.0))
         left.append(jnp.concatenate(columns, axis=0))
         right.append(one_hot_rows(node, nodes))
@@ -134,7 +165,7 @@
     sums = lax.dot_general(both, right, NT, preferred_element_type=jnp.float32)
     sums = sums[:40] + sums[40:]
     for m in range(9):
-        nodes_ref[m] = sums[4 * m : 4 * m + 3]
+        (dom_far_ref, dom_near_ref, own_ref)[m // 3][m % 3] = sums[4 * m : 4 * m + 4]
 
 
 def solve(arrived, inverse, connectivity, node_count):
@@ -143,16 +174,23 @@
         solve_kernel,
         out_shape=(
             jax.ShapeDtypeStruct((12, 1, cells), jnp.float32),
-            jax.ShapeDtypeStruct((9, 3, node_count), jnp.float32),
-        ),
+        )
+        + (jax.ShapeDtypeStruct((3, 4, node_count), jnp.float32),) * 3,
         compiler_params=pltpu.CompilerParams(vmem_limit_bytes=48 * 1024 * 1024),
         name="solve",
     )(arrived, inverse, connectivity)
 
 
-def shifted(array, axis, by):
+def swap_near(array, axis):
     devices = lax.axis_size(axis)
-    pairs = [(i, i + by) for i in range(devices) if 0 <= i + by < devices]
+    return lax.ppermute(array, axis, [(i, i ^ 1) for i in range(devices)])
+
+
+def swap_far(array, axis, close):
+    devices = lax.axis_size(axis)
+    pairs = [(i, ((i + 1) ^ 1) - 1) for i in range(1, devices - 1)]
+    if close:
+        pairs = [(0, devices - 1)] + pairs + [(devices - 1, 0)]
     return lax.ppermute(array, axis, pairs)
 
 
@@ -164,11 +202,10 @@
     owner = owner_dom.reshape(1, particles)
     sums = partial_sums(basis_weights, velocity, owner, cell_local, doms, cells)
     arrived = lax.all_to_all(sums, "dom", split_axis=0, concat_axis=0, tiled=True)
-    coefficients, local = solve(arrived, inverse, connectivity, nodes)
-    local = local.reshape(3, 3, 3, nodes)
-    merged = local[:, 1] + shifted(local[:, 2], "dom", 1) + shifted(local[:, 0], "dom", -1)
-    total = merged[1] + shifted(merged[2], "slab", 1) + shifted(merged[0], "slab", -1)
-    return coefficients, total.reshape(3, 1, nodes)
+    coefficients, dom_far, dom_near, own = solve(arrived, inverse, connectivity, nodes)
+    merged = own + swap_far(dom_far, "dom", False) + swap_near(dom_near, "dom")
+    total = merged[2] + swap_far(merged[0], "slab", True) + swap_near(merged[1], "slab")
+    return coefficients, total[:3].reshape(3, 1, nodes)
 
 
 def solution(mesh):

time: 37.4 us -> 27.5 us (0.74)
  the two profiles are of different devices: /device:TPU:1 before, /device:TPU:9 now
where the time goes in v2:
time: 27.5 us; the launch traced here: 27.3 us
  starting transfers between devices  10.6 us (39%)
  blocking collectives  10.4 us (38%)
  waiting for transfers between devices  2.96 us (11%)
  Pallas kernels  2.02 us (7%)
  between operations  0.67 us (2%)
  local copies, waits for them, and re-layouts  0.6 us (2%)
    all_to_all x1, blocking collectives, per_device(): lax.all_to_all(sums, 'dom', split_axis=0, concat_axis=0, tiled=True)  10.4 us
    ppermute x2, starting transfers between devices, swap_near(): return lax.ppermute(array, axis, [(i, i ^ 1) for i in range(devices)])  6.3 us
    ppermute x2, starting transfers between devices, swap_far(): return lax.ppermute(array, axis, pairs)  4.28 us
    ppermute x2, waiting for transfers between devices, swap_far(): return lax.ppermute(array, axis, pairs)  2.58 us
    pallas_call x1, Pallas kernels, partial_sums(): pl.pallas_call(partial_sums_kernel, grid=(dom_count // DOM_BLOCK,), in_sp...  1.3 us
    pallas_call x1, Pallas kernels, solve(): pl.pallas_call(solve_kernel, out_shape=(jax.ShapeDtypeStruct((12, 1, cell...  0.73 us
    unnamed x5, local copies, waits for them, and re-layouts  0.6 us
  transfers between devices with their start and end apart: 4, of which 3 were waited for; matrix products, arithmetic and copies ran while one was open for 0% of the time, Pallas kernels for 0%

profile of v2, /device:TPU:9, one launch (start us, length us, event | category | flops | bytes accessed | tf_op | source)
XLA Modules:
  0.0 27.3 jit_solution(6457501173134409079)
XLA Ops:
  0.6 1.3 %partial_sums.1 = f32[8,24,256]{2,1,0:T(8,128)S(1)} custom-call(f32[4,1,1536]{2,1,0:T(1,128)} %weights_hbm.1, f32[3,1,1536]{2,1,0:T(1,128)} %velocity_hbm.1, s32[1,1536]{1,0:T(1,128)} %bitcast.9, s32[1,1536]{1,0:T(1,128)} %cell_hbm.1), custom_call_target="tpu_custom_call" | custom-call | tf_op jit(solution)/shard_map/partial_sums/pallas_call | solution.py:82
  1.9 0.0 copy-start
  1.9 0.0 copy-start.1
  2.0 10.4 %all_to_all.5.arrived_ref = f32[8,24,256]{2,1,0:T(8,128)S(1)} all-to-all(f32[8,24,256]{2,1,0:T(8,128)S(1)} %partial_sums.1), channel_id=1, replica_groups=mesh['dom'=8,'slab'=4] {'dom'}, dimensions={0} | all-to-all | bytes 393216 | tf_op jit(solution)/shard_map/all_to_all | solution.py:204
  12.4 0.0 copy-done
  12.4 0.0 copy-done.1
  12.4 0.7 %solve.1 = (f32[12,1,256]{2,1,0:T(1,128)}, f32[3,4,256]{2,1,0:T(4,128)S(1)}, f32[3,4,256]{2,1,0:T(4,128)S(1)}, f32[3,4,256]{2,1,0:T(4,128)S(1)}) custom-call(f32[8,24,256]{2,1,0:T(8,128)S(1)} %all_to_all.5.arrived_ref, f32[16,1,256]{2,1,0:T(1,128)S(1)} %copy-done, s32[4,1,256]{2,1,0:T(1,128)S(1)} %copy-done.1), custom_call_target="tpu_custom_call" | custom-call | tf_op jit(solution)/shard_map/solve/pallas_call | solution.py:173
  13.1 3.1 %collective-permute-start = (f32[3,4,256]{2,1,0:T(4,128)S(1)}, f32[3,4,256]{2,1,0:T(4,128)S(1)}, u32[]{:S(2)}, u32[]{:S(2)}) collective-permute-start(f32[3,4,256]{2,1,0:T(4,128)S(1)} %get-tuple-element.8), channel_id=1, source_target_pairs={{4,8},{8,4},{12,16},{16,12},{20,24},{24,20},{5,9},{9,5},{13,17},{1... | collective-permute-start | bytes 36872 | tf_op jit(solution)/shard_map/ppermute | solution.py:194
  16.2 1.5 %collective-permute-start.1 = (f32[3,4,256]{2,1,0:T(4,128)S(1)}, f32[3,4,256]{2,1,0:T(4,128)S(1)}, u32[]{:S(2)}, u32[]{:S(2)}) collective-permute-start(f32[3,4,256]{2,1,0:T(4,128)S(1)} %get-tuple-element.9), channel_id=1, source_target_pairs={{0,4},{4,0},{8,12},{12,8},{16,20},{20,16},{24,28},{28,24},{1,5},{5... | collective-permute-start | bytes 36872 | tf_op jit(solution)/shard_map/ppermute | solution.py:186
  17.7 0.7 %collective-permute-done = f32[3,4,256]{2,1,0:T(4,128)S(1)} collective-permute-done((f32[3,4,256]{2,1,0:T(4,128)S(1)}, f32[3,4,256]{2,1,0:T(4,128)S(1)}, u32[]{:S(2)}, u32[]{:S(2)}) %collective-permute-start) | collective-permute-done | bytes 12320 | tf_op jit(solution)/shard_map/ppermute | solution.py:194
  18.4 0.4 %collective-permute-done.1 = f32[3,4,256]{2,1,0:T(4,128)S(1)} collective-permute-done((f32[3,4,256]{2,1,0:T(4,128)S(1)}, f32[3,4,256]{2,1,0:T(4,128)S(1)}, u32[]{:S(2)}, u32[]{:S(2)}) %collective-permute-start.1) | collective-permute-done | bytes 12320 | tf_op jit(solution)/shard_map/ppermute | solution.py:186
  18.8 4.8 %collective-permute-start.3 = (f32[4,256]{1,0:T(4,128)S(1)}, f32[4,256]{1,0:T(4,128)S(1)}, u32[]{:S(2)}, u32[]{:S(2)}) collective-permute-start(f32[4,256]{1,0:T(4,128)S(1)} %get-tuple-element.13), channel_id=1, source_target_pairs={{0,1},{1,0},{2,3},{3,2},{4,5},{5,4},{6,7},{7,6},{8,9},{9,8},{10,11... | collective-permute-start | bytes 12296 | tf_op jit(solution)/shard_map/ppermute | solution.py:186
  23.6 1.2 %collective-permute-start.2 = (f32[4,256]{1,0:T(4,128)S(1)}, f32[4,256]{1,0:T(4,128)S(1)}, u32[]{:S(2)}, u32[]{:S(2)}) collective-permute-start(f32[4,256]{1,0:T(4,128)S(1)} %get-tuple-element.14), channel_id=1, source_target_pairs={{0,3},{1,2},{2,1},{3,0},{4,7},{5,6},{6,5},{7,4},{8,11},{9,10},{10,... | collective-permute-start | bytes 12296 | tf_op jit(solution)/shard_map/ppermute | solution.py:194
  24.8 0.0 collective-permute-done.3
  24.8 1.8 %collective-permute-done.2 = f32[4,256]{1,0:T(4,128)S(1)} collective-permute-done((f32[4,256]{1,0:T(4,128)S(1)}, f32[4,256]{1,0:T(4,128)S(1)}, u32[]{:S(2)}, u32[]{:S(2)}) %collective-permute-start.2) | collective-permute-done | bytes 4128 | tf_op jit(solution)/shard_map/ppermute | solution.py:194
  26.7 0.6 %copy.8 = f32[3,1,256]{2,1,0:T(1,128)} copy(f32[3,1,256]{2,0,1:T(4,128)S(1)} %fusion) | data formatting | bytes 6144
  (3 shorter events, 0.0 us)
Async XLA Ops:
  1.9 10.4 %copy-start = (f32[16,1,256]{2,1,0:T(1,128)S(1)}, f32[16,1,256]{2,1,0:T(1,128)}, u32[]{:S(2)}) copy-start(f32[16,1,256]{2,1,0:T(1,128)} %inverse_ref.1) | copy-start | bytes 49156
  1.9 10.4 %copy-start.1 = (s32[4,1,256]{2,1,0:T(1,128)S(1)}, s32[4,1,256]{2,1,0:T(1,128)}, u32[]{:S(2)}) copy-start(s32[4,1,256]{2,1,0:T(1,128)} %connectivity_ref.1) | copy-start | bytes 12292
  13.1 5.3 %collective-permute-start = (f32[3,4,256]{2,1,0:T(4,128)S(1)}, f32[3,4,256]{2,1,0:T(4,128)S(1)}, u32[]{:S(2)}, u32[]{:S(2)}) collective-permute-start(f32[3,4,256]{2,1,0:T(4,128)S(1)} %get-tuple-element.8), channel_id=1, source_target_pairs={{4,8},{8,4},{12,16},{16,12},{20,24},{24,20},{5,9},{9,5},{13,17},{1... | collective-permute-start | bytes 36872 | tf_op jit(solution)/shard_map/ppermute | solution.py:194
  16.2 2.6 %collective-permute-start.1 = (f32[3,4,256]{2,1,0:T(4,128)S(1)}, f32[3,4,256]{2,1,0:T(4,128)S(1)}, u32[]{:S(2)}, u32[]{:S(2)}) collective-permute-start(f32[3,4,256]{2,1,0:T(4,128)S(1)} %get-tuple-element.9), channel_id=1, source_target_pairs={{0,4},{4,0},{8,12},{12,8},{16,20},{20,16},{24,28},{28,24},{1,5},{5... | collective-permute-start | bytes 36872 | tf_op jit(solution)/shard_map/ppermute | solution.py:186
  18.8 6.0 %collective-permute-start.3 = (f32[4,256]{1,0:T(4,128)S(1)}, f32[4,256]{1,0:T(4,128)S(1)}, u32[]{:S(2)}, u32[]{:S(2)}) collective-permute-start(f32[4,256]{1,0:T(4,128)S(1)} %get-tuple-element.13), channel_id=1, source_target_pairs={{0,1},{1,0},{2,3},{3,2},{4,5},{5,4},{6,7},{7,6},{8,9},{9,8},{10,11... | collective-permute-start | bytes 12296 | tf_op jit(solution)/shard_map/ppermute | solution.py:186
  23.6 3.0 %collective-permute-start.2 = (f32[4,256]{1,0:T(4,128)S(1)}, f32[4,256]{1,0:T(4,128)S(1)}, u32[]{:S(2)}, u32[]{:S(2)}) collective-permute-start(f32[4,256]{1,0:T(4,128)S(1)} %get-tuple-element.14), channel_id=1, source_target_pairs={{0,3},{1,2},{2,1},{3,0},{4,7},{5,6},{6,5},{7,4},{8,11},{9,10},{10,... | collective-permute-start | bytes 12296 | tf_op jit(solution)/shard_map/ppermute | solution.py:194

commit v3 on v2

--- a/solution.py
+++ b/solution.py
@@ -186,12 +186,21 @@
     return lax.ppermute(array, axis, [(i, i ^ 1) for i in range(devices)])
 
 
-def swap_far(array, axis, close):
-    devices = lax.axis_size(axis)
-    pairs = [(i, ((i + 1) ^ 1) - 1) for i in range(1, devices - 1)]
-    if close:
-        pairs = [(0, devices - 1)] + pairs + [(devices - 1, 0)]
-    return lax.ppermute(array, axis, pairs)
+def swap_far_slab(array):
+    slabs = lax.axis_size("slab")
+    pairs = [(i, ((i + 1) ^ 1) - 1) for i in range(1, slabs - 1)]
+    return lax.ppermute(array, "slab", [(0, slabs - 1)] + pairs + [(slabs - 1, 0)])
+
+
+def swap_far_dom(array):
+    doms, slabs = lax.axis_size("dom"), lax.axis_size("slab")
+    pairs = []
+    for d in range(doms):
+        for s in range(slabs):
+            inside = 0 < d < doms - 1
+            to = (((d + 1) ^ 1) - 1) * slabs + s if inside else d * slabs + (s ^ 1)
+            pairs.append((d * slabs + s, to))
+    return lax.ppermute(array, ("dom", "slab"), pairs)
 
 
 def per_device(basis_weights, velocity, owner_dom, cell_local, inverse, connectivity):
@@ -203,8 +212,8 @@
     sums = partial_sums(basis_weights, velocity, owner, cell_local, doms, cells)
     arrived = lax.all_to_all(sums, "dom", split_axis=0, concat_axis=0, tiled=True)
     coefficients, dom_far, dom_near, own = solve(arrived, inverse, connectivity, nodes)
-    merged = own + swap_far(dom_far, "dom", False) + swap_near(dom_near, "dom")
-    total = merged[2] + swap_far(merged[0], "slab", True) + swap_near(merged[1], "slab")
+    merged = own + swap_far_dom(dom_far) + swap_near(dom_near, "dom")
+    total = merged[2] + swap_far_slab(merged[0]) + swap_near(merged[1], "slab")
     return coefficients, total[:3].reshape(3, 1, nodes)
 
 

time: 27.5 us -> 25.5 us (0.927)
  the two profiles are of different devices: /device:TPU:9 before, /device:TPU:0 now
where the time goes in v3:
time: 25.5 us; the launch traced here: 25.2 us
  blocking collectives  15 us (59%)
  starting transfers between devices  3.46 us (14%)
  waiting for transfers between devices  3.41 us (13%)
  Pallas kernels  2.02 us (8%)
  between operations  0.67 us (3%)
  local copies, waits for them, and re-layouts  0.6 us (2%)
    all_to_all x1, blocking collectives, per_device(): lax.all_to_all(sums, 'dom', split_axis=0, concat_axis=0, tiled=True)  15 us
    ppermute x2, waiting for transfers between devices, swap_near(): return lax.ppermute(array, axis, [(i, i ^ 1) for i in range(devices)])  1.94 us
    ppermute x2, starting transfers between devices, swap_near(): return lax.ppermute(array, axis, [(i, i ^ 1) for i in range(devices)])  1.82 us
    ppermute x1, starting transfers between devices, swap_far_slab(): lax.ppermute(array, 'slab', [(0, slabs - 1)] + pairs + [(slabs - 1, 0)])  1.63 us
    ppermute x1, waiting for transfers between devices, swap_far_slab(): lax.ppermute(array, 'slab', [(0, slabs - 1)] + pairs + [(slabs - 1, 0)])  1.46 us
    pallas_call x1, Pallas kernels, partial_sums(): pl.pallas_call(partial_sums_kernel, grid=(dom_count // DOM_BLOCK,), in_sp...  1.3 us
    pallas_call x1, Pallas kernels, solve(): pl.pallas_call(solve_kernel, out_shape=(jax.ShapeDtypeStruct((12, 1, cell...  0.73 us
    unnamed x5, local copies, waits for them, and re-layouts  0.6 us
  transfers between devices with their start and end apart: 4, of which 2 were waited for; matrix products, arithmetic and copies ran while one was open for 0% of the time, Pallas kernels for 0%

profile of v3, /device:TPU:0, one launch (start us, length us, event | category | flops | bytes accessed | tf_op | source)
XLA Modules:
  0.0 25.2 jit_solution(15746540752071589752)
XLA Ops:
  0.6 1.3 %partial_sums.1 = f32[8,24,256]{2,1,0:T(8,128)S(1)} custom-call(f32[4,1,1536]{2,1,0:T(1,128)} %weights_hbm.1, f32[3,1,1536]{2,1,0:T(1,128)} %velocity_hbm.1, s32[1,1536]{1,0:T(1,128)} %bitcast.9, s32[1,1536]{1,0:T(1,128)} %cell_hbm.1), custom_call_target="tpu_custom_call" | custom-call | tf_op jit(solution)/shard_map/partial_sums/pallas_call | solution.py:82
  1.9 0.0 copy-start
  1.9 0.0 copy-start.1
  2.0 15.0 %all_to_all.5.arrived_ref = f32[8,24,256]{2,1,0:T(8,128)S(1)} all-to-all(f32[8,24,256]{2,1,0:T(8,128)S(1)} %partial_sums.1), channel_id=1, replica_groups=mesh['dom'=8,'slab'=4] {'dom'}, dimensions={0} | all-to-all | bytes 393216 | tf_op jit(solution)/shard_map/all_to_all | solution.py:213
  17.0 0.0 copy-done
  17.0 0.0 copy-done.1
  17.0 0.7 %solve.1 = (f32[12,1,256]{2,1,0:T(1,128)}, f32[3,4,256]{2,1,0:T(4,128)S(1)}, f32[3,4,256]{2,1,0:T(4,128)S(1)}, f32[3,4,256]{2,1,0:T(4,128)S(1)}) custom-call(f32[8,24,256]{2,1,0:T(8,128)S(1)} %all_to_all.5.arrived_ref, f32[16,1,256]{2,1,0:T(1,128)S(1)} %copy-done, s32[4,1,256]{2,1,0:T(1,128)S(1)} %copy-done.1), custom_call_target="tpu_custom_call" | custom-call | tf_op jit(solution)/shard_map/solve/pallas_call | solution.py:173
  17.7 0.0 collective-permute-start
  17.7 1.7 %collective-permute-start.1 = (f32[3,4,256]{2,1,0:T(4,128)S(1)}, f32[3,4,256]{2,1,0:T(4,128)S(1)}, u32[]{:S(2)}, u32[]{:S(2)}) collective-permute-start(f32[3,4,256]{2,1,0:T(4,128)S(1)} %get-tuple-element.9), channel_id=1, source_target_pairs={{0,4},{4,0},{8,12},{12,8},{16,20},{20,16},{24,28},{28,24},{1,5},{5... | collective-permute-start | bytes 36872 | tf_op jit(solution)/shard_map/ppermute | solution.py:186
  19.4 0.0 collective-permute-done
  19.4 1.9 %collective-permute-done.1 = f32[3,4,256]{2,1,0:T(4,128)S(1)} collective-permute-done((f32[3,4,256]{2,1,0:T(4,128)S(1)}, f32[3,4,256]{2,1,0:T(4,128)S(1)}, u32[]{:S(2)}, u32[]{:S(2)}) %collective-permute-start.1) | collective-permute-done | bytes 12320 | tf_op jit(solution)/shard_map/ppermute | solution.py:186
  21.4 0.1 collective-permute-start.3
  21.5 1.6 %collective-permute-start.2 = (f32[4,256]{1,0:T(4,128)S(1)}, f32[4,256]{1,0:T(4,128)S(1)}, u32[]{:S(2)}, u32[]{:S(2)}) collective-permute-start(f32[4,256]{1,0:T(4,128)S(1)} %get-tuple-element.14), channel_id=1, source_target_pairs={{0,3},{1,2},{2,1},{3,0},{4,7},{5,6},{6,5},{7,4},{8,11},{9,10},{10,... | collective-permute-start | bytes 12296 | tf_op jit(solution)/shard_map/ppermute | solution.py:192
  23.1 0.0 collective-permute-done.3
  23.1 1.5 %collective-permute-done.2 = f32[4,256]{1,0:T(4,128)S(1)} collective-permute-done((f32[4,256]{1,0:T(4,128)S(1)}, f32[4,256]{1,0:T(4,128)S(1)}, u32[]{:S(2)}, u32[]{:S(2)}) %collective-permute-start.2) | collective-permute-done | bytes 4128 | tf_op jit(solution)/shard_map/ppermute | solution.py:192
  24.6 0.6 %copy.8 = f32[3,1,256]{2,1,0:T(1,128)} copy(f32[3,1,256]{2,0,1:T(4,128)S(1)} %fusion) | data formatting | bytes 6144
  (3 shorter events, 0.0 us)
Async XLA Ops:
  1.9 15.0 %copy-start = (f32[16,1,256]{2,1,0:T(1,128)S(1)}, f32[16,1,256]{2,1,0:T(1,128)}, u32[]{:S(2)}) copy-start(f32[16,1,256]{2,1,0:T(1,128)} %inverse_ref.1) | copy-start | bytes 49156
  1.9 15.0 %copy-start.1 = (s32[4,1,256]{2,1,0:T(1,128)S(1)}, s32[4,1,256]{2,1,0:T(1,128)}, u32[]{:S(2)}) copy-start(s32[4,1,256]{2,1,0:T(1,128)} %connectivity_ref.1) | copy-start | bytes 12292
  17.7 1.8 %collective-permute-start = (f32[3,4,256]{2,1,0:T(4,128)S(1)}, f32[3,4,256]{2,1,0:T(4,128)S(1)}, u32[]{:S(2)}, u32[]{:S(2)}) collective-permute-start(f32[3,4,256]{2,1,0:T(4,128)S(1)} %get-tuple-element.8), channel_id=1, source_target_pairs={{0,1},{1,0},{2,3},{3,2},{4,8},{5,9},{6,10},{7,11},{8,4},{9,5},{10,... | collective-permute-start | bytes 36872 | tf_op jit(solution)/shard_map/ppermute | solution.py:203
  17.7 3.7 %collective-permute-start.1 = (f32[3,4,256]{2,1,0:T(4,128)S(1)}, f32[3,4,256]{2,1,0:T(4,128)S(1)}, u32[]{:S(2)}, u32[]{:S(2)}) collective-permute-start(f32[3,4,256]{2,1,0:T(4,128)S(1)} %get-tuple-element.9), channel_id=1, source_target_pairs={{0,4},{4,0},{8,12},{12,8},{16,20},{20,16},{24,28},{28,24},{1,5},{5... | collective-permute-start | bytes 36872 | tf_op jit(solution)/shard_map/ppermute | solution.py:186
  21.4 1.7 %collective-permute-start.3 = (f32[4,256]{1,0:T(4,128)S(1)}, f32[4,256]{1,0:T(4,128)S(1)}, u32[]{:S(2)}, u32[]{:S(2)}) collective-permute-start(f32[4,256]{1,0:T(4,128)S(1)} %get-tuple-element.13), channel_id=1, source_target_pairs={{0,1},{1,0},{2,3},{3,2},{4,5},{5,4},{6,7},{7,6},{8,9},{9,8},{10,11... | collective-permute-start | bytes 12296 | tf_op jit(solution)/shard_map/ppermute | solution.py:186
  21.5 3.1 %collective-permute-start.2 = (f32[4,256]{1,0:T(4,128)S(1)}, f32[4,256]{1,0:T(4,128)S(1)}, u32[]{:S(2)}, u32[]{:S(2)}) collective-permute-start(f32[4,256]{1,0:T(4,128)S(1)} %get-tuple-element.14), channel_id=1, source_target_pairs={{0,3},{1,2},{2,1},{3,0},{4,7},{5,6},{6,5},{7,4},{8,11},{9,10},{10,... | collective-permute-start | bytes 12296 | tf_op jit(solution)/shard_map/ppermute | solution.py:192

commit v4 on v3

--- a/solution.py
+++ b/solution.py
@@ -17,8 +17,17 @@
 
 
 def one_hot_rows(index_row, count):
-    rows = lax.broadcasted_iota(jnp.int32, (count, index_row.shape[1]), 0)
-    return jnp.where(rows == index_row, 1.0, 0.0).astype(jnp.bfloat16)
+    lanes = 128
+    rows = lax.broadcasted_iota(jnp.int32, (count, lanes), 0).astype(jnp.bfloat16)
+    index = index_row.astype(jnp.float32).astype(jnp.bfloat16)
+    one, zero = jnp.bfloat16(1), jnp.bfloat16(0)
+    return jnp.concatenate(
+        [
+            jnp.where(rows == index[:, at : at + lanes], one, zero)
+            for at in range(0, index_row.shape[1], lanes)
+        ],
+        axis=1,
+    )
 
 
 def partial_sums_kernel(
@@ -139,9 +148,9 @@
         first = apply(inverse_columns, moment)
         residual = moment - apply(gram_columns, first)
         solved.append(first + apply(inverse_columns, residual))
-    for i in range(4):
-        for a in range(3):
-            coefficients_ref[3 * i + a] = solved[a][i : i + 1]
+    coefficients_ref[...] = jnp.concatenate(
+        [solved[a][i : i + 1] for i in range(4) for a in range(3)], axis=0
+    )
     left, right = [], []
     for k in range(4):
         values = jnp.concatenate(
@@ -173,7 +182,7 @@
     return pl.pallas_call(
         solve_kernel,
         out_shape=(
-            jax.ShapeDtypeStruct((12, 1, cells), jnp.float32),
+            jax.ShapeDtypeStruct((12, cells), jnp.float32),
         )
         + (jax.ShapeDtypeStruct((3, 4, node_count), jnp.float32),) * 3,
         compiler_params=pltpu.CompilerParams(vmem_limit_bytes=48 * 1024 * 1024),
@@ -213,8 +222,8 @@
     arrived = lax.all_to_all(sums, "dom", split_axis=0, concat_axis=0, tiled=True)
     coefficients, dom_far, dom_near, own = solve(arrived, inverse, connectivity, nodes)
     merged = own + swap_far_dom(dom_far) + swap_near(dom_near, "dom")
-    total = merged[2] + swap_far_slab(merged[0]) + swap_near(merged[1], "slab")
-    return coefficients, total[:3].reshape(3, 1, nodes)
+    total = merged[2] + swap_near(merged[1], "slab") + swap_far_slab(merged[0])
+    return coefficients.reshape(12, 1, cells), total[:3].reshape(3, 1, nodes)
 
 
 def solution(mesh):

time: 25.5 us -> 25.1 us (0.984)
  local copies, waits for them, and re-layouts: 0.6 us -> 1.22 us
  waiting for transfers between devices: 3.41 us -> 2.8 us
  Pallas kernels: 2.02 us -> 1.62 us
    ppermute x1, starting transfers between devices: 1.63 us -> 0.49 us  [swap_far_slab(): lax.ppermute(array, 'slab', [(0, slabs - 1)] + pairs + [(slabs - 1, 0)])]
    ppermute x2, starting transfers between devices: 1.82 us -> 2.95 us  [swap_near(): return lax.ppermute(array, axis, [(i, i ^ 1) for i in range(devices)])]
    ppermute x1, waiting for transfers between devices: 1.46 us -> 0.78 us  [swap_far_slab(): lax.ppermute(array, 'slab', [(0, slabs - 1)] + pairs + [(slabs - 1, 0)])]
    unnamed x5 -> x6, local copies, waits for them, and re-layouts: 0.6 us -> 1.21 us
    pallas_call x1, Pallas kernels: 0.73 us -> 0.33 us  [solve(): pl.pallas_call(solve_kernel, out_shape=(jax.ShapeDtypeStruct((12, cells),...]
  transfers between devices with their start and end apart: 4 -> 4, of which waited for: 2 -> 2; matrix products, arithmetic and copies ran while one was open for 0% -> 2% of each run, Pallas kernels for 0% -> 0%
where the time goes in v4:
time: 25.1 us; the launch traced here: 24.8 us
  blocking collectives  15 us (60%)
  starting transfers between devices  3.52 us (14%)
  waiting for transfers between devices  2.8 us (11%)
  Pallas kernels  1.62 us (6%)
  local copies, waits for them, and re-layouts  1.22 us (5%)
  between operations  0.67 us (3%)
    all_to_all x1, blocking collectives, per_device(): lax.all_to_all(sums, 'dom', split_axis=0, concat_axis=0, tiled=True)  15 us
    ppermute x2, starting transfers between devices, swap_near(): return lax.ppermute(array, axis, [(i, i ^ 1) for i in range(devices)])  2.95 us
    ppermute x2, waiting for transfers between devices, swap_near(): return lax.ppermute(array, axis, [(i, i ^ 1) for i in range(devices)])  2.02 us
    pallas_call x1, Pallas kernels, partial_sums(): pl.pallas_call(partial_sums_kernel, grid=(dom_count // DOM_BLOCK,), in_sp...  1.3 us
    unnamed x6, local copies, waits for them, and re-layouts  1.21 us
    ppermute x1, waiting for transfers between devices, swap_far_slab(): lax.ppermute(array, 'slab', [(0, slabs - 1)] + pairs + [(slabs - 1, 0)])  0.78 us
  transfers between devices with their start and end apart: 4, of which 2 were waited for; matrix products, arithmetic and copies ran while one was open for 2% of the time, Pallas kernels for 0%

profile of v4, /device:TPU:0, one launch (start us, length us, event | category | flops | bytes accessed | tf_op | source)
XLA Modules:
  0.0 24.8 jit_solution(5666562145399727368)
XLA Ops:
  0.6 1.3 %partial_sums.1 = f32[8,24,256]{2,1,0:T(8,128)S(1)} custom-call(f32[4,1,1536]{2,1,0:T(1,128)} %weights_hbm.1, f32[3,1,1536]{2,1,0:T(1,128)} %velocity_hbm.1, s32[1,1536]{1,0:T(1,128)} %bitcast.11, s32[1,1536]{1,0:T(1,128)} %cell_hbm.1), custom_call_target="tpu_custom_call" | custom-call | tf_op jit(solution)/shard_map/partial_sums/pallas_call | solution.py:91
  1.9 0.0 copy-start
  1.9 0.0 copy-start.1
  2.0 15.0 %all_to_all.5.arrived_ref = f32[8,24,256]{2,1,0:T(8,128)S(1)} all-to-all(f32[8,24,256]{2,1,0:T(8,128)S(1)} %partial_sums.1), channel_id=1, replica_groups=mesh['dom'=8,'slab'=4] {'dom'}, dimensions={0} | all-to-all | bytes 393216 | tf_op jit(solution)/shard_map/all_to_all | solution.py:222
  17.0 0.0 copy-done
  17.0 0.0 copy-done.1
  17.0 0.3 %solve.1 = (f32[12,256]{1,0:T(8,128)S(1)}, f32[3,4,256]{2,1,0:T(4,128)S(1)}, f32[3,4,256]{2,1,0:T(4,128)S(1)}, f32[3,4,256]{2,1,0:T(4,128)S(1)}) custom-call(f32[8,24,256]{2,1,0:T(8,128)S(1)} %all_to_all.5.arrived_ref, f32[16,1,256]{2,1,0:T(1,128)S(1)} %copy-done, s32[4,1,256]{2,1,0:T(1,128)S(1)} %copy-done.1), custom_call_target="tpu_custom_call" | custom-call | tf_op jit(solution)/shard_map/solve/pallas_call | solution.py:182
  17.3 0.1 collective-permute-start
  17.4 1.7 %collective-permute-start.1 = (f32[3,4,256]{2,1,0:T(4,128)S(1)}, f32[3,4,256]{2,1,0:T(4,128)S(1)}, u32[]{:S(2)}, u32[]{:S(2)}) collective-permute-start(f32[3,4,256]{2,1,0:T(4,128)S(1)} %get-tuple-element.9), channel_id=1, source_target_pairs={{0,4},{4,0},{8,12},{12,8},{16,20},{20,16},{24,28},{28,24},{1,5},{5... | collective-permute-start | bytes 36872 | tf_op jit(solution)/shard_map/ppermute | solution.py:195
  19.1 0.0 collective-permute-done
  19.1 2.0 %collective-permute-done.1 = f32[3,4,256]{2,1,0:T(4,128)S(1)} collective-permute-done((f32[3,4,256]{2,1,0:T(4,128)S(1)}, f32[3,4,256]{2,1,0:T(4,128)S(1)}, u32[]{:S(2)}, u32[]{:S(2)}) %collective-permute-start.1) | collective-permute-done | bytes 12320 | tf_op jit(solution)/shard_map/ppermute | solution.py:195
  21.1 0.5 %collective-permute-start.3 = (f32[4,256]{1,0:T(4,128)S(1)}, f32[4,256]{1,0:T(4,128)S(1)}, u32[]{:S(2)}, u32[]{:S(2)}) collective-permute-start(f32[4,256]{1,0:T(4,128)S(1)} %get-tuple-element.13), channel_id=1, source_target_pairs={{0,3},{1,2},{2,1},{3,0},{4,7},{5,6},{6,5},{7,4},{8,11},{9,10},{10,... | collective-permute-start | bytes 12296 | tf_op jit(solution)/shard_map/ppermute | solution.py:201
  21.6 1.2 %collective-permute-start.2 = (f32[4,256]{1,0:T(4,128)S(1)}, f32[4,256]{1,0:T(4,128)S(1)}, u32[]{:S(2)}, u32[]{:S(2)}) collective-permute-start(f32[4,256]{1,0:T(4,128)S(1)} %get-tuple-element.14), channel_id=1, source_target_pairs={{0,1},{1,0},{2,3},{3,2},{4,5},{5,4},{6,7},{7,6},{8,9},{9,8},{10,11... | collective-permute-start | bytes 12296 | tf_op jit(solution)/shard_map/ppermute | solution.py:195
  22.8 0.6 %copy.8 = f32[12,1,256]{2,1,0:T(1,128)} copy(f32[12,1,256]{2,0,1:T(8,128)S(1)} %bitcast.10) | data formatting | bytes 24576
  23.5 0.8 %collective-permute-done.3 = f32[4,256]{1,0:T(4,128)S(1)} collective-permute-done((f32[4,256]{1,0:T(4,128)S(1)}, f32[4,256]{1,0:T(4,128)S(1)}, u32[]{:S(2)}, u32[]{:S(2)}) %collective-permute-start.3) | collective-permute-done | bytes 4128 | tf_op jit(solution)/shard_map/ppermute | solution.py:201
  24.2 0.0 collective-permute-done.2
  24.2 0.6 %copy.9 = f32[3,1,256]{2,1,0:T(1,128)} copy(f32[3,1,256]{2,0,1:T(4,128)S(1)} %fusion) | data formatting | bytes 6144
  (3 shorter events, 0.0 us)
Async XLA Ops:
  1.9 15.0 %copy-start = (f32[16,1,256]{2,1,0:T(1,128)S(1)}, f32[16,1,256]{2,1,0:T(1,128)}, u32[]{:S(2)}) copy-start(f32[16,1,256]{2,1,0:T(1,128)} %inverse_ref.1) | copy-start | bytes 49156
  1.9 15.0 %copy-start.1 = (s32[4,1,256]{2,1,0:T(1,128)S(1)}, s32[4,1,256]{2,1,0:T(1,128)}, u32[]{:S(2)}) copy-start(s32[4,1,256]{2,1,0:T(1,128)} %connectivity_ref.1) | copy-start | bytes 12292
  17.3 1.8 %collective-permute-start = (f32[3,4,256]{2,1,0:T(4,128)S(1)}, f32[3,4,256]{2,1,0:T(4,128)S(1)}, u32[]{:S(2)}, u32[]{:S(2)}) collective-permute-start(f32[3,4,256]{2,1,0:T(4,128)S(1)} %get-tuple-element.8), channel_id=1, source_target_pairs={{0,1},{1,0},{2,3},{3,2},{4,8},{5,9},{6,10},{7,11},{8,4},{9,5},{10,... | collective-permute-start | bytes 36872 | tf_op jit(solution)/shard_map/ppermute | solution.py:212
  17.4 3.8 %collective-permute-start.1 = (f32[3,4,256]{2,1,0:T(4,128)S(1)}, f32[3,4,256]{2,1,0:T(4,128)S(1)}, u32[]{:S(2)}, u32[]{:S(2)}) collective-permute-start(f32[3,4,256]{2,1,0:T(4,128)S(1)} %get-tuple-element.9), channel_id=1, source_target_pairs={{0,4},{4,0},{8,12},{12,8},{16,20},{20,16},{24,28},{28,24},{1,5},{5... | collective-permute-start | bytes 36872 | tf_op jit(solution)/shard_map/ppermute | solution.py:195
  21.1 3.1 %collective-permute-start.3 = (f32[4,256]{1,0:T(4,128)S(1)}, f32[4,256]{1,0:T(4,128)S(1)}, u32[]{:S(2)}, u32[]{:S(2)}) collective-permute-start(f32[4,256]{1,0:T(4,128)S(1)} %get-tuple-element.13), channel_id=1, source_target_pairs={{0,3},{1,2},{2,1},{3,0},{4,7},{5,6},{6,5},{7,4},{8,11},{9,10},{10,... | collective-permute-start | bytes 12296 | tf_op jit(solution)/shard_map/ppermute | solution.py:201
  21.6 2.6 %collective-permute-start.2 = (f32[4,256]{1,0:T(4,128)S(1)}, f32[4,256]{1,0:T(4,128)S(1)}, u32[]{:S(2)}, u32[]{:S(2)}) collective-permute-start(f32[4,256]{1,0:T(4,128)S(1)} %get-tuple-element.14), channel_id=1, source_target_pairs={{0,1},{1,0},{2,3},{3,2},{4,5},{5,4},{6,7},{7,6},{8,9},{9,8},{10,11... | collective-permute-start | bytes 12296 | tf_op jit(solution)/shard_map/ppermute | solution.py:195

commit v5 on v4

--- a/solution.py
+++ b/solution.py
@@ -7,6 +7,8 @@
 
 DOM_BLOCK = 8
 TERMS = 24
+SENT_BY_EVEN = (6, 0, 4, 3)
+SENT_BY_ODD = (7, 1, 5, 2)
 NT = (((1,), (1,)), ((), ()))
 
 
@@ -30,30 +32,7 @@
     )
 
 
-def partial_sums_kernel(
-    weights_hbm, velocity_hbm, owner_hbm, cell_hbm, sums_ref,
-    weights_ref, velocity_ref, owner_ref, cell_ref, arrivals,
-):
-    pairs = (
-        (weights_hbm, weights_ref),
-        (velocity_hbm, velocity_ref),
-        (owner_hbm, owner_ref),
-        (cell_hbm, cell_ref),
-    )
-
-    @pl.when(pl.program_id(0) == 0)
-    def _():
-        copies = [
-            pltpu.make_async_copy(source, target, arrivals.at[i])
-            for i, (source, target) in enumerate(pairs)
-        ]
-        for copy in copies:
-            copy.start()
-        for copy in copies:
-            copy.wait()
-
-    cell_count = sums_ref.shape[2]
-    first_dom = pl.program_id(0) * DOM_BLOCK
+def sums_by_owner(weights_ref, velocity_ref, owner_ref, cell_ref, doms, cell_count):
     w = weights_ref[:, 0, :]
     v = velocity_ref[:, 0, :]
     particles = w.shape[1]
@@ -75,51 +54,85 @@
     both = jnp.concatenate([high, low], axis=0)
     owner = owner_ref[...]
     picked = []
-    for d in range(DOM_BLOCK):
-        named = jnp.where(owner == first_dom + d, 1.0, 0.0).astype(jnp.bfloat16)
+    for dom in doms:
+        named = jnp.where(owner == dom, 1.0, 0.0).astype(jnp.bfloat16)
         picked.append(both * named)
     left = jnp.concatenate(picked, axis=0)
     right = one_hot_rows(cell_ref[...], cell_count)
     sums = lax.dot_general(left, right, NT, preferred_element_type=jnp.float32)
-    for d in range(DOM_BLOCK):
-        at = 2 * TERMS * d
-        sums_ref[d] = sums[at : at + TERMS] + sums[at + TERMS : at + 2 * TERMS]
-
-
-def partial_sums(basis_weights, velocity, owner, cell_local, dom_count, cell_count):
-    particles = cell_local.shape[1]
+    for j in range(len(doms)):
+        at = 2 * TERMS * j
+        yield sums[at : at + TERMS] + sums[at + TERMS : at + 2 * TERMS]
+
+
+def fetch(pairs, arrivals):
+    copies = [
+        pltpu.make_async_copy(source, target, arrivals.at[i])
+        for i, (source, target) in enumerate(pairs)
+    ]
+    for copy in copies:
+        copy.start()
+    for copy in copies:
+        copy.wait()
+
+
+def few_doms_kernel(*refs):
+    sources, (keep_ref, give_ref), held, arrivals = refs[:4], refs[4:6], refs[6:10], refs[10]
+    fetch(list(zip(sources, held)), arrivals)
+    me = lax.axis_index("dom")
+    odd = lax.rem(lax.axis_index("slab"), 2)
+    pairs = list(zip(SENT_BY_EVEN, SENT_BY_ODD))
+    doms = [me ^ (e + odd * (o - e)) for e, o in pairs]
+    doms += [me ^ (o + odd * (e - o)) for e, o in pairs]
+    for k, sums in enumerate(sums_by_owner(*held, doms, keep_ref.shape[2])):
+        (keep_ref, give_ref)[k // 4][k % 4] = sums
+
+
+def many_doms_kernel(*refs):
+    sources, sums_ref, held, arrivals = refs[:4], refs[4], refs[5:9], refs[9]
+
+    @pl.when(pl.program_id(0) == 0)
+    def _():
+        fetch(list(zip(sources, held)), arrivals)
+
+    first = pl.program_id(0) * DOM_BLOCK
+    doms = [first + k for k in range(DOM_BLOCK)]
+    for k, sums in enumerate(sums_by_owner(*held, doms, sums_ref.shape[2])):
+        sums_ref[k] = sums
+
+
+def partial_sums(arrays, dom_count, cell_count):
+    few = dom_count == DOM_BLOCK
+    if few:
+        out_shape = [jax.ShapeDtypeStruct((4, TERMS, cell_count), jnp.float32)] * 2
+        out_specs = [pl.BlockSpec((4, TERMS, cell_count), lambda i: (0, 0, 0))] * 2
+    else:
+        out_specs = pl.BlockSpec((DOM_BLOCK, TERMS, cell_count), lambda i: (i, 0, 0))
+        out_shape = jax.ShapeDtypeStruct((dom_count, TERMS, cell_count), jnp.float32)
     return pl.pallas_call(
-        partial_sums_kernel,
+        few_doms_kernel if few else many_doms_kernel,
         grid=(dom_count // DOM_BLOCK,),
-        in_specs=[pl.BlockSpec(memory_space=pltpu.HBM)] * 4,
-        out_specs=pl.BlockSpec((DOM_BLOCK, TERMS, cell_count), lambda i: (i, 0, 0)),
-        out_shape=jax.ShapeDtypeStruct((dom_count, TERMS, cell_count), jnp.float32),
-        scratch_shapes=[
-            pltpu.VMEM((4, 1, particles), jnp.float32),
-            pltpu.VMEM((3, 1, particles), jnp.float32),
-            pltpu.VMEM((1, particles), jnp.int32),
-            pltpu.VMEM((1, particles), jnp.int32),
-            pltpu.SemaphoreType.DMA((4,)),
-        ],
+        in_specs=[pl.BlockSpec(memory_space=pltpu.HBM)] * len(arrays),
+        out_specs=out_specs,
+        out_shape=out_shape,
+        scratch_shapes=[pltpu.VMEM(a.shape, a.dtype) for a in arrays]
+        + [pltpu.SemaphoreType.DMA((len(arrays),))],
         compiler_params=pltpu.CompilerParams(vmem_limit_bytes=48 * 1024 * 1024),
         name="partial_sums",
-    )(*(pltpu.with_memory_space_constraint(a, pltpu.HBM) for a in (basis_weights, velocity, owner, cell_local)))
-
-
-def solve_kernel(
-    arrived_ref, inverse_ref, connectivity_ref,
-    coefficients_ref, dom_far_ref, dom_near_ref, own_ref,
-):
-    cells = arrived_ref.shape[2]
+    )(*(pltpu.with_memory_space_constraint(a, pltpu.HBM) for a in arrays))
+
+
+def solve_kernel(*refs):
+    blocks, (inverse_ref, connectivity_ref) = refs[:-6], refs[-6:-4]
+    coefficients_ref, dom_far_ref, dom_near_ref, own_ref = refs[-4:]
+    cells = inverse_ref.shape[2]
     nodes = own_ref.shape[2]
     dom_odd = lax.rem(lax.axis_index("dom"), 2)
     slab_odd = lax.rem(lax.axis_index("slab"), 2)
     dom_moves = (2 * dom_odd, 2 - 2 * dom_odd, 1)
     slab_moves = (2 * slab_odd, 2 - 2 * slab_odd, 1)
     wanted = [3 * slab_move + dom_move for dom_move in dom_moves for slab_move in slab_moves]
-    total = arrived_ref[0]
-    for d in range(1, arrived_ref.shape[0]):
-        total = total + arrived_ref[d]
+    total = sum(block[d] for block in blocks for d in range(block.shape[0]))
 
     def gram(i, j):
         if i == j:
@@ -177,8 +190,8 @@
         (dom_far_ref, dom_near_ref, own_ref)[m // 3][m % 3] = sums[4 * m : 4 * m + 4]
 
 
-def solve(arrived, inverse, connectivity, node_count):
-    cells = arrived.shape[2]
+def solve(blocks, inverse, connectivity, node_count):
+    cells = inverse.shape[2]
     return pl.pallas_call(
         solve_kernel,
         out_shape=(
@@ -187,29 +200,45 @@
         + (jax.ShapeDtypeStruct((3, 4, node_count), jnp.float32),) * 3,
         compiler_params=pltpu.CompilerParams(vmem_limit_bytes=48 * 1024 * 1024),
         name="solve",
-    )(arrived, inverse, connectivity)
-
-
-def swap_near(array, axis):
-    devices = lax.axis_size(axis)
-    return lax.ppermute(array, axis, [(i, i ^ 1) for i in range(devices)])
-
-
-def swap_far_slab(array):
-    slabs = lax.axis_size("slab")
-    pairs = [(i, ((i + 1) ^ 1) - 1) for i in range(1, slabs - 1)]
-    return lax.ppermute(array, "slab", [(0, slabs - 1)] + pairs + [(slabs - 1, 0)])
-
-
-def swap_far_dom(array):
+    )(*blocks, inverse, connectivity)
+
+
+def send(array, dom_step, slab_step):
     doms, slabs = lax.axis_size("dom"), lax.axis_size("slab")
     pairs = []
     for d in range(doms):
         for s in range(slabs):
-            inside = 0 < d < doms - 1
-            to = (((d + 1) ^ 1) - 1) * slabs + s if inside else d * slabs + (s ^ 1)
-            pairs.append((d * slabs + s, to))
+            to_dom, to_slab = dom_step(d, s), slab_step(s) % slabs
+            if not 0 <= to_dom < doms:
+                to_dom, to_slab = d, s ^ 1
+            pairs.append((d * slabs + s, to_dom * slabs + to_slab))
     return lax.ppermute(array, ("dom", "slab"), pairs)
+
+
+def stay(i, s=0):
+    return i
+
+
+def near(i, s=0):
+    return i ^ 1
+
+
+def far(i, s=0):
+    return ((i + 1) ^ 1) - 1
+
+
+def to_owners(sums):
+    if not isinstance(sums, (list, tuple)):
+        return [lax.all_to_all(sums, "dom", split_axis=0, concat_axis=0, tiled=True)]
+    keep, give = sums
+    other = send(give, stay, near)
+    arrived = []
+    for j in range(4):
+        both = jnp.concatenate([keep[j], other[j]], axis=0)
+        step = lambda d, s, j=j: d ^ (SENT_BY_ODD if s % 2 else SENT_BY_EVEN)[j]
+        arrived.append(send(both, step, near))
+    total = (arrived[0] + arrived[1]) + (arrived[2] + arrived[3])
+    return [total[None, TERMS:], send(total[:TERMS], stay, near)[None]]
 
 
 def per_device(basis_weights, velocity, owner_dom, cell_local, inverse, connectivity):
@@ -218,11 +247,10 @@
     nodes = 256
     doms = lax.axis_size("dom")
     owner = owner_dom.reshape(1, particles)
-    sums = partial_sums(basis_weights, velocity, owner, cell_local, doms, cells)
-    arrived = lax.all_to_all(sums, "dom", split_axis=0, concat_axis=0, tiled=True)
-    coefficients, dom_far, dom_near, own = solve(arrived, inverse, connectivity, nodes)
-    merged = own + swap_far_dom(dom_far) + swap_near(dom_near, "dom")
-    total = merged[2] + swap_near(merged[1], "slab") + swap_far_slab(merged[0])
+    sums = partial_sums((basis_weights, velocity, owner, cell_local), doms, cells)
+    coefficients, dom_far, dom_near, own = solve(to_owners(sums), inverse, connectivity, nodes)
+    merged = own + send(dom_far, far, stay) + send(dom_near, near, stay)
+    total = merged[2] + send(merged[1], stay, near) + send(merged[0], stay, far)
     return coefficients.reshape(12, 1, cells), total[:3].reshape(3, 1, nodes)
 
 

time: 25.1 us -> 23.7 us (0.944)
  blocking collectives: 15 us -> 0 us
  starting transfers between devices: 3.52 us -> 12 us
  waiting for transfers between devices: 2.8 us -> 8 us
    all_to_all x1 -> x0, blocking collectives: 15 us -> none  [per_device(): lax.all_to_all(sums, 'dom', split_axis=0, concat_axis=0, tiled=True)]
    ppermute x4 -> x10, starting transfers between devices: 3.52 us -> 12 us  [send(): return lax.ppermute(array, ('dom', 'slab'), pairs)]
    ppermute x4 -> x10, waiting for transfers between devices: 2.8 us -> 8 us  [send(): return lax.ppermute(array, ('dom', 'slab'), pairs)]
  transfers between devices with their start and end apart: 4 -> 10, of which waited for: 2 -> 7; matrix products, arithmetic and copies ran while one was open for 2% -> 3% of each run, Pallas kernels for 0% -> 0%
where the time goes in v5:
time: 23.7 us; the launch traced here: 23.6 us
  starting transfers between devices  12 us (51%)
  waiting for transfers between devices  8 us (34%)
  Pallas kernels  1.62 us (7%)
  local copies, waits for them, and re-layouts  1.24 us (5%)
  between operations  0.68 us (3%)
    ppermute x10, starting transfers between devices, send(): return lax.ppermute(array, ('dom', 'slab'), pairs)  12 us
    ppermute x10, waiting for transfers between devices, send(): return lax.ppermute(array, ('dom', 'slab'), pairs)  8 us
    pallas_call x1, Pallas kernels, partial_sums(): pl.pallas_call(few_doms_kernel if few else many_doms_kernel, grid=(dom_co...  1.31 us
    unnamed x6, local copies, waits for them, and re-layouts  1.21 us
  transfers between devices with their start and end apart: 10, of which 7 were waited for; matrix products, arithmetic and copies ran while one was open for 3% of the time, Pallas kernels for 0%

profile of v5, /device:TPU:0, one launch (start us, length us, event | category | flops | bytes accessed | tf_op | source)
XLA Modules:
  0.0 23.6 jit_solution(10626813419361010413)
XLA Ops:
  0.6 1.3 %partial_sums.1 = (f32[4,24,256]{2,1,0:T(8,128)S(1)}, f32[4,24,256]{2,1,0:T(8,128)S(1)}) custom-call(f32[4,1,1536]{2,1,0:T(1,128)} %refs_0_.1, f32[3,1,1536]{2,1,0:T(1,128)} %refs_1_.1, s32[1,1536]{1,0:T(1,128)} %bitcast.31, s32[1,1536]{1,0:T(1,128)} %refs_3_.2), custom_call_target="tpu_custom_call" | custom-call | tf_op jit(solution)/shard_map/partial_sums/pallas_call | solution.py:112
  1.9 0.5 %collective-permute-start = (f32[4,24,256]{2,1,0:T(8,128)S(1)}, f32[4,24,256]{2,1,0:T(8,128)S(1)}, u32[]{:S(2)}, u32[]{:S(2)}) collective-permute-start(f32[4,24,256]{2,1,0:T(8,128)S(1)} %get-tuple-element.9), channel_id=1, source_target_pairs={{0,1},{1,0},{2,3},{3,2},{4,5},{5,4},{6,7},{7,6},{8,9},{9,8},{10,11... | collective-permute-start | bytes 294920 | tf_op jit(solution)/shard_map/ppermute | solution.py:215
  2.5 0.9 %collective-permute-done = f32[4,24,256]{2,1,0:T(8,128)S(1)} collective-permute-done((f32[4,24,256]{2,1,0:T(8,128)S(1)}, f32[4,24,256]{2,1,0:T(8,128)S(1)}, u32[]{:S(2)}, u32[]{:S(2)}) %collective-permute-start) | collective-permute-done | bytes 98336 | tf_op jit(solution)/shard_map/ppermute | solution.py:215
  3.4 4.8 %collective-permute-start.1 = (f32[48,256]{1,0:T(8,128)S(1)}, f32[48,256]{1,0:T(8,128)S(1)}, u32[]{:S(2)}, u32[]{:S(2)}) collective-permute-start(f32[48,256]{1,0:T(8,128)S(1)} %pad_maximum_fusion), channel_id=1, source_target_pairs={{0,25},{1,28},{2,27},{3,30},{4,29},{5,24},{6,31},{7,26},{8,17},{9,... | collective-permute-start | bytes 147464 | tf_op jit(solution)/shard_map/ppermute | solution.py:215
  8.2 0.3 %collective-permute-start.3 = (f32[48,256]{1,0:T(8,128)S(1)}, f32[48,256]{1,0:T(8,128)S(1)}, u32[]{:S(2)}, u32[]{:S(2)}) collective-permute-start(f32[48,256]{1,0:T(8,128)S(1)} %pad_maximum_fusion.2), channel_id=1, source_target_pairs={{0,17},{1,20},{2,19},{3,22},{4,21},{5,16},{6,23},{7,18},{8,25},{9,... | collective-permute-start | bytes 147464 | tf_op jit(solution)/shard_map/ppermute | solution.py:215
  8.5 1.2 %collective-permute-start.4 = (f32[48,256]{1,0:T(8,128)S(1)}, f32[48,256]{1,0:T(8,128)S(1)}, u32[]{:S(2)}, u32[]{:S(2)}) collective-permute-start(f32[48,256]{1,0:T(8,128)S(1)} %pad_maximum_fusion.3), channel_id=1, source_target_pairs={{0,13},{1,8},{2,15},{3,10},{4,9},{5,12},{6,11},{7,14},{8,5},{9,0},... | collective-permute-start | bytes 147464 | tf_op jit(solution)/shard_map/ppermute | solution.py:215
  9.7 0.3 %collective-permute-start.2 = (f32[48,256]{1,0:T(8,128)S(1)}, f32[48,256]{1,0:T(8,128)S(1)}, u32[]{:S(2)}, u32[]{:S(2)}) collective-permute-start(f32[48,256]{1,0:T(8,128)S(1)} %pad_maximum_fusion.1), channel_id=1, source_target_pairs={{0,1},{1,4},{2,3},{3,6},{4,5},{5,0},{6,7},{7,2},{8,9},{9,12},{10,1... | collective-permute-start | bytes 147464 | tf_op jit(solution)/shard_map/ppermute | solution.py:215
  10.0 1.0 %collective-permute-done.1 = f32[48,256]{1,0:T(8,128)S(1)} collective-permute-done((f32[48,256]{1,0:T(8,128)S(1)}, f32[48,256]{1,0:T(8,128)S(1)}, u32[]{:S(2)}, u32[]{:S(2)}) %collective-permute-start.1) | collective-permute-done | bytes 49184 | tf_op jit(solution)/shard_map/ppermute | solution.py:215
  11.0 2.7 %collective-permute-done.3 = f32[48,256]{1,0:T(8,128)S(1)} collective-permute-done((f32[48,256]{1,0:T(8,128)S(1)}, f32[48,256]{1,0:T(8,128)S(1)}, u32[]{:S(2)}, u32[]{:S(2)}) %collective-permute-start.3) | collective-permute-done | bytes 49184 | tf_op jit(solution)/shard_map/ppermute | solution.py:215
  13.7 0.0 collective-permute-done.4
  13.7 0.1 collective-permute-done.2
  13.8 0.0 copy-start
  13.8 0.0 copy-start.1
  13.8 0.7 %collective-permute-start.5 = (f32[24,256]{1,0:T(8,128)S(1)}, f32[24,256]{1,0:T(8,128)S(1)}, u32[]{:S(2)}, u32[]{:S(2)}) collective-permute-start(f32[24,256]{1,0:T(8,128)S(1)} %get-tuple-element.24), channel_id=1, source_target_pairs={{0,1},{1,0},{2,3},{3,2},{4,5},{5,4},{6,7},{7,6},{8,9},{9,8},{10,11... | collective-permute-start | bytes 73736 | tf_op jit(solution)/shard_map/ppermute | solution.py:215
  14.6 0.8 %collective-permute-done.5 = f32[24,256]{1,0:T(8,128)S(1)} collective-permute-done((f32[24,256]{1,0:T(8,128)S(1)}, f32[24,256]{1,0:T(8,128)S(1)}, u32[]{:S(2)}, u32[]{:S(2)}) %collective-permute-start.5) | collective-permute-done | bytes 24608 | tf_op jit(solution)/shard_map/ppermute | solution.py:215
  15.4 0.0 copy-done
  15.4 0.0 copy-done.1
  15.4 0.3 %solve.1 = (f32[12,256]{1,0:T(8,128)S(1)}, f32[3,4,256]{2,1,0:T(4,128)S(1)}, f32[3,4,256]{2,1,0:T(4,128)S(1)}, f32[3,4,256]{2,1,0:T(4,128)S(1)}) custom-call(f32[1,24,256]{2,1,0:T(8,128)S(1)} %get-tuple-element.25.refs_0_, f32[1,24,256]{2,1,0:T(8,128)S(1)} %bitcast.29, f32[16,1,256]{2,1,0:T(1,128)S(1)} %copy-done, s32[4,1,256]{2,1,0:T(1,128)S(1)} %copy-done.1), custom_call_target="tpu_custom_call" | custom-call | tf_op jit(solution)/shard_map/solve/pallas_call | solution.py:195
  15.7 0.4 %collective-permute-start.6 = (f32[3,4,256]{2,1,0:T(4,128)S(1)}, f32[3,4,256]{2,1,0:T(4,128)S(1)}, u32[]{:S(2)}, u32[]{:S(2)}) collective-permute-start(f32[3,4,256]{2,1,0:T(4,128)S(1)} %get-tuple-element.12), channel_id=1, source_target_pairs={{0,1},{1,0},{2,3},{3,2},{4,8},{5,9},{6,10},{7,11},{8,4},{9,5},{10,... | collective-permute-start | bytes 36872 | tf_op jit(solution)/shard_map/ppermute | solution.py:215
  16.1 2.0 %collective-permute-start.7 = (f32[3,4,256]{2,1,0:T(4,128)S(1)}, f32[3,4,256]{2,1,0:T(4,128)S(1)}, u32[]{:S(2)}, u32[]{:S(2)}) collective-permute-start(f32[3,4,256]{2,1,0:T(4,128)S(1)} %get-tuple-element.13), channel_id=1, source_target_pairs={{0,4},{1,5},{2,6},{3,7},{4,0},{5,1},{6,2},{7,3},{8,12},{9,13},{10,... | collective-permute-start | bytes 36872 | tf_op jit(solution)/shard_map/ppermute | solution.py:215
  18.2 0.0 collective-permute-done.6
  18.2 1.7 %collective-permute-done.7 = f32[3,4,256]{2,1,0:T(4,128)S(1)} collective-permute-done((f32[3,4,256]{2,1,0:T(4,128)S(1)}, f32[3,4,256]{2,1,0:T(4,128)S(1)}, u32[]{:S(2)}, u32[]{:S(2)}) %collective-permute-start.7) | collective-permute-done | bytes 12320 | tf_op jit(solution)/shard_map/ppermute | solution.py:215
  19.9 0.4 %collective-permute-start.9 = (f32[4,256]{1,0:T(4,128)S(1)}, f32[4,256]{1,0:T(4,128)S(1)}, u32[]{:S(2)}, u32[]{:S(2)}) collective-permute-start(f32[4,256]{1,0:T(4,128)S(1)} %get-tuple-element.27), channel_id=1, source_target_pairs={{0,3},{1,2},{2,1},{3,0},{4,7},{5,6},{6,5},{7,4},{8,11},{9,10},{10,... | collective-permute-start | bytes 12296 | tf_op jit(solution)/shard_map/ppermute | solution.py:215
  20.2 1.3 %collective-permute-start.8 = (f32[4,256]{1,0:T(4,128)S(1)}, f32[4,256]{1,0:T(4,128)S(1)}, u32[]{:S(2)}, u32[]{:S(2)}) collective-permute-start(f32[4,256]{1,0:T(4,128)S(1)} %get-tuple-element.28), channel_id=1, source_target_pairs={{0,1},{1,0},{2,3},{3,2},{4,5},{5,4},{6,7},{7,6},{8,9},{9,8},{10,11... | collective-permute-start | bytes 12296 | tf_op jit(solution)/shard_map/ppermute | solution.py:215
  21.6 0.6 %copy.8 = f32[12,1,256]{2,1,0:T(1,128)} copy(f32[12,1,256]{2,0,1:T(8,128)S(1)} %bitcast.30) | data formatting | bytes 24576
  22.2 0.8 %collective-permute-done.9 = f32[4,256]{1,0:T(4,128)S(1)} collective-permute-done((f32[4,256]{1,0:T(4,128)S(1)}, f32[4,256]{1,0:T(4,128)S(1)}, u32[]{:S(2)}, u32[]{:S(2)}) %collective-permute-start.9) | collective-permute-done | bytes 4128 | tf_op jit(solution)/shard_map/ppermute | solution.py:215
  23.0 0.0 collective-permute-done.8
  23.0 0.6 %copy.9 = f32[3,1,256]{2,1,0:T(1,128)} copy(f32[3,1,256]{2,0,1:T(4,128)S(1)} %fusion) | data formatting | bytes 6144
  (11 shorter events, 0.1 us)
Async XLA Ops:
  1.9 1.5 %collective-permute-start = (f32[4,24,256]{2,1,0:T(8,128)S(1)}, f32[4,24,256]{2,1,0:T(8,128)S(1)}, u32[]{:S(2)}, u32[]{:S(2)}) collective-permute-start(f32[4,24,256]{2,1,0:T(8,128)S(1)} %get-tuple-element.9), channel_id=1, source_target_pairs={{0,1},{1,0},{2,3},{3,2},{4,5},{5,4},{6,7},{7,6},{8,9},{9,8},{10,11... | collective-permute-start | bytes 294920 | tf_op jit(solution)/shard_map/ppermute | solution.py:215
  3.4 7.6 %collective-permute-start.1 = (f32[48,256]{1,0:T(8,128)S(1)}, f32[48,256]{1,0:T(8,128)S(1)}, u32[]{:S(2)}, u32[]{:S(2)}) collective-permute-start(f32[48,256]{1,0:T(8,128)S(1)} %pad_maximum_fusion), channel_id=1, source_target_pairs={{0,25},{1,28},{2,27},{3,30},{4,29},{5,24},{6,31},{7,26},{8,17},{9,... | collective-permute-start | bytes 147464 | tf_op jit(solution)/shard_map/ppermute | solution.py:215
  8.2 5.5 %collective-permute-start.3 = (f32[48,256]{1,0:T(8,128)S(1)}, f32[48,256]{1,0:T(8,128)S(1)}, u32[]{:S(2)}, u32[]{:S(2)}) collective-permute-start(f32[48,256]{1,0:T(8,128)S(1)} %pad_maximum_fusion.2), channel_id=1, source_target_pairs={{0,17},{1,20},{2,19},{3,22},{4,21},{5,16},{6,23},{7,18},{8,25},{9,... | collective-permute-start | bytes 147464 | tf_op jit(solution)/shard_map/ppermute | solution.py:215
  8.5 5.1 %collective-permute-start.4 = (f32[48,256]{1,0:T(8,128)S(1)}, f32[48,256]{1,0:T(8,128)S(1)}, u32[]{:S(2)}, u32[]{:S(2)}) collective-permute-start(f32[48,256]{1,0:T(8,128)S(1)} %pad_maximum_fusion.3), channel_id=1, source_target_pairs={{0,13},{1,8},{2,15},{3,10},{4,9},{5,12},{6,11},{7,14},{8,5},{9,0},... | collective-permute-start | bytes 147464 | tf_op jit(solution)/shard_map/ppermute | solution.py:215
  9.7 4.1 %collective-permute-start.2 = (f32[48,256]{1,0:T(8,128)S(1)}, f32[48,256]{1,0:T(8,128)S(1)}, u32[]{:S(2)}, u32[]{:S(2)}) collective-permute-start(f32[48,256]{1,0:T(8,128)S(1)} %pad_maximum_fusion.1), channel_id=1, source_target_pairs={{0,1},{1,4},{2,3},{3,6},{4,5},{5,0},{6,7},{7,2},{8,9},{9,12},{10,1... | collective-permute-start | bytes 147464 | tf_op jit(solution)/shard_map/ppermute | solution.py:215
  13.8 1.6 %copy-start = (f32[16,1,256]{2,1,0:T(1,128)S(1)}, f32[16,1,256]{2,1,0:T(1,128)}, u32[]{:S(2)}) copy-start(f32[16,1,256]{2,1,0:T(1,128)} %refs_2_.1) | copy-start | bytes 49156
  13.8 1.6 %copy-start.1 = (s32[4,1,256]{2,1,0:T(1,128)S(1)}, s32[4,1,256]{2,1,0:T(1,128)}, u32[]{:S(2)}) copy-start(s32[4,1,256]{2,1,0:T(1,128)} %refs_3_.3) | copy-start | bytes 12292
  13.8 1.6 %collective-permute-start.5 = (f32[24,256]{1,0:T(8,128)S(1)}, f32[24,256]{1,0:T(8,128)S(1)}, u32[]{:S(2)}, u32[]{:S(2)}) collective-permute-start(f32[24,256]{1,0:T(8,128)S(1)} %get-tuple-element.24), channel_id=1, source_target_pairs={{0,1},{1,0},{2,3},{3,2},{4,5},{5,4},{6,7},{7,6},{8,9},{9,8},{10,11... | collective-permute-start | bytes 73736 | tf_op jit(solution)/shard_map/ppermute | solution.py:215
  15.7 2.4 %collective-permute-start.6 = (f32[3,4,256]{2,1,0:T(4,128)S(1)}, f32[3,4,256]{2,1,0:T(4,128)S(1)}, u32[]{:S(2)}, u32[]{:S(2)}) collective-permute-start(f32[3,4,256]{2,1,0:T(4,128)S(1)} %get-tuple-element.12), channel_id=1, source_target_pairs={{0,1},{1,0},{2,3},{3,2},{4,8},{5,9},{6,10},{7,11},{8,4},{9,5},{10,... | collective-permute-start | bytes 36872 | tf_op jit(solution)/shard_map/ppermute | solution.py:215
  16.1 3.7 %collective-permute-start.7 = (f32[3,4,256]{2,1,0:T(4,128)S(1)}, f32[3,4,256]{2,1,0:T(4,128)S(1)}, u32[]{:S(2)}, u32[]{:S(2)}) collective-permute-start(f32[3,4,256]{2,1,0:T(4,128)S(1)} %get-tuple-element.13), channel_id=1, source_target_pairs={{0,4},{1,5},{2,6},{3,7},{4,0},{5,1},{6,2},{7,3},{8,12},{9,13},{10,... | collective-permute-start | bytes 36872 | tf_op jit(solution)/shard_map/ppermute | solution.py:215
  19.9 3.1 %collective-permute-start.9 = (f32[4,256]{1,0:T(4,128)S(1)}, f32[4,256]{1,0:T(4,128)S(1)}, u32[]{:S(2)}, u32[]{:S(2)}) collective-permute-start(f32[4,256]{1,0:T(4,128)S(1)} %get-tuple-element.27), channel_id=1, source_target_pairs={{0,3},{1,2},{2,1},{3,0},{4,7},{5,6},{6,5},{7,4},{8,11},{9,10},{10,... | collective-permute-start | bytes 12296 | tf_op jit(solution)/shard_map/ppermute | solution.py:215
  20.2 2.7 %collective-permute-start.8 = (f32[4,256]{1,0:T(4,128)S(1)}, f32[4,256]{1,0:T(4,128)S(1)}, u32[]{:S(2)}, u32[]{:S(2)}) collective-permute-start(f32[4,256]{1,0:T(4,128)S(1)} %get-tuple-element.28), channel_id=1, source_target_pairs={{0,1},{1,0},{2,3},{3,2},{4,5},{5,4},{6,7},{7,6},{8,9},{9,8},{10,11... | collective-permute-start | bytes 12296 | tf_op jit(solution)/shard_map/ppermute | solution.py:215

commit v6 on v5

--- a/solution.py
+++ b/solution.py
@@ -7,8 +7,8 @@
 
 DOM_BLOCK = 8
 TERMS = 24
-SENT_BY_EVEN = (6, 0, 4, 3)
-SENT_BY_ODD = (7, 1, 5, 2)
+SENT_BY_EVEN = (6, 1, 4, 3)
+SENT_BY_ODD = (7, 0, 5, 2)
 NT = (((1,), (1,)), ((), ()))
 
 
@@ -227,6 +227,10 @@
     return ((i + 1) ^ 1) - 1
 
 
+def far_of_near(i):
+    return far(near(i))
+
+
 def to_owners(sums):
     if not isinstance(sums, (list, tuple)):
         return [lax.all_to_all(sums, "dom", split_axis=0, concat_axis=0, tiled=True)]
@@ -249,8 +253,8 @@
     owner = owner_dom.reshape(1, particles)
     sums = partial_sums((basis_weights, velocity, owner, cell_local), doms, cells)
     coefficients, dom_far, dom_near, own = solve(to_owners(sums), inverse, connectivity, nodes)
-    merged = own + send(dom_far, far, stay) + send(dom_near, near, stay)
-    total = merged[2] + send(merged[1], stay, near) + send(merged[0], stay, far)
+    merged = send(dom_near, near, near) + send(dom_far, far, near) + send(own, stay, near)
+    total = merged[1] + send(merged[2], stay, near) + send(merged[0], stay, far_of_near)
     return coefficients.reshape(12, 1, cells), total[:3].reshape(3, 1, nodes)
 
 

time: 23.7 us -> 23.4 us (0.987)
  starting transfers between devices: 12 us -> 11.2 us
  waiting for transfers between devices: 8 us -> 8.37 us
    ppermute x10 -> x11, starting transfers between devices: 12 us -> 11.2 us  [send(): return lax.ppermute(array, ('dom', 'slab'), pairs)]
    ppermute x10 -> x11, waiting for transfers between devices: 8 us -> 8.37 us  [send(): return lax.ppermute(array, ('dom', 'slab'), pairs)]
  transfers between devices with their start and end apart: 10 -> 11, of which waited for: 7 -> 6; matrix products, arithmetic and copies ran while one was open for 3% -> 3% of each run, Pallas kernels for 0% -> 0%
where the time goes in v6:
time: 23.4 us; the launch traced here: 23.2 us
  starting transfers between devices  11.2 us (48%)
  waiting for transfers between devices  8.37 us (36%)
  Pallas kernels  1.63 us (7%)
  local copies, waits for them, and re-layouts  1.23 us (5%)
  between operations  0.7 us (3%)
    ppermute x11, starting transfers between devices, send(): return lax.ppermute(array, ('dom', 'slab'), pairs)  11.2 us
    ppermute x11, waiting for transfers between devices, send(): return lax.ppermute(array, ('dom', 'slab'), pairs)  8.37 us
    pallas_call x1, Pallas kernels, partial_sums(): pl.pallas_call(few_doms_kernel if few else many_doms_kernel, grid=(dom_co...  1.31 us
    unnamed x6, local copies, waits for them, and re-layouts  1.21 us
  transfers between devices with their start and end apart: 11, of which 6 were waited for; matrix products, arithmetic and copies ran while one was open for 3% of the time, Pallas kernels for 0%

profile of v6, /device:TPU:0, one launch (start us, length us, event | category | flops | bytes accessed | tf_op | source)
XLA Modules:
  0.0 23.2 jit_solution(18237138987164737726)
XLA Ops:
  0.6 1.3 %partial_sums.1 = (f32[4,24,256]{2,1,0:T(8,128)S(1)}, f32[4,24,256]{2,1,0:T(8,128)S(1)}) custom-call(f32[4,1,1536]{2,1,0:T(1,128)} %refs_0_.1, f32[3,1,1536]{2,1,0:T(1,128)} %refs_1_.1, s32[1,1536]{1,0:T(1,128)} %bitcast.31, s32[1,1536]{1,0:T(1,128)} %refs_3_.2), custom_call_target="tpu_custom_call" | custom-call | tf_op jit(solution)/shard_map/partial_sums/pallas_call | solution.py:112
  1.9 0.5 %collective-permute-start = (f32[4,24,256]{2,1,0:T(8,128)S(1)}, f32[4,24,256]{2,1,0:T(8,128)S(1)}, u32[]{:S(2)}, u32[]{:S(2)}) collective-permute-start(f32[4,24,256]{2,1,0:T(8,128)S(1)} %get-tuple-element.9), channel_id=1, source_target_pairs={{0,1},{1,0},{2,3},{3,2},{4,5},{5,4},{6,7},{7,6},{8,9},{9,8},{10,11... | collective-permute-start | bytes 294920 | tf_op jit(solution)/shard_map/ppermute | solution.py:215
  2.5 0.9 %collective-permute-done = f32[4,24,256]{2,1,0:T(8,128)S(1)} collective-permute-done((f32[4,24,256]{2,1,0:T(8,128)S(1)}, f32[4,24,256]{2,1,0:T(8,128)S(1)}, u32[]{:S(2)}, u32[]{:S(2)}) %collective-permute-start) | collective-permute-done | bytes 98336 | tf_op jit(solution)/shard_map/ppermute | solution.py:215
  3.4 4.8 %collective-permute-start.1 = (f32[48,256]{1,0:T(8,128)S(1)}, f32[48,256]{1,0:T(8,128)S(1)}, u32[]{:S(2)}, u32[]{:S(2)}) collective-permute-start(f32[48,256]{1,0:T(8,128)S(1)} %pad_maximum_fusion), channel_id=1, source_target_pairs={{0,25},{1,28},{2,27},{3,30},{4,29},{5,24},{6,31},{7,26},{8,17},{9,... | collective-permute-start | bytes 147464 | tf_op jit(solution)/shard_map/ppermute | solution.py:215
  8.2 0.3 %collective-permute-start.3 = (f32[48,256]{1,0:T(8,128)S(1)}, f32[48,256]{1,0:T(8,128)S(1)}, u32[]{:S(2)}, u32[]{:S(2)}) collective-permute-start(f32[48,256]{1,0:T(8,128)S(1)} %pad_maximum_fusion.2), channel_id=1, source_target_pairs={{0,17},{1,20},{2,19},{3,22},{4,21},{5,16},{6,23},{7,18},{8,25},{9,... | collective-permute-start | bytes 147464 | tf_op jit(solution)/shard_map/ppermute | solution.py:215
  8.5 1.2 %collective-permute-start.4 = (f32[48,256]{1,0:T(8,128)S(1)}, f32[48,256]{1,0:T(8,128)S(1)}, u32[]{:S(2)}, u32[]{:S(2)}) collective-permute-start(f32[48,256]{1,0:T(8,128)S(1)} %pad_maximum_fusion.3), channel_id=1, source_target_pairs={{0,13},{1,8},{2,15},{3,10},{4,9},{5,12},{6,11},{7,14},{8,5},{9,0},... | collective-permute-start | bytes 147464 | tf_op jit(solution)/shard_map/ppermute | solution.py:215
  9.7 0.3 %collective-permute-start.2 = (f32[48,256]{1,0:T(8,128)S(1)}, f32[48,256]{1,0:T(8,128)S(1)}, u32[]{:S(2)}, u32[]{:S(2)}) collective-permute-start(f32[48,256]{1,0:T(8,128)S(1)} %pad_maximum_fusion.1), channel_id=1, source_target_pairs={{0,5},{1,0},{2,7},{3,2},{4,1},{5,4},{6,3},{7,6},{8,13},{9,8},{10,1... | collective-permute-start | bytes 147464 | tf_op jit(solution)/shard_map/ppermute | solution.py:215
  10.0 0.9 %collective-permute-done.1 = f32[48,256]{1,0:T(8,128)S(1)} collective-permute-done((f32[48,256]{1,0:T(8,128)S(1)}, f32[48,256]{1,0:T(8,128)S(1)}, u32[]{:S(2)}, u32[]{:S(2)}) %collective-permute-start.1) | collective-permute-done | bytes 49184 | tf_op jit(solution)/shard_map/ppermute | solution.py:215
  11.0 2.7 %collective-permute-done.3 = f32[48,256]{1,0:T(8,128)S(1)} collective-permute-done((f32[48,256]{1,0:T(8,128)S(1)}, f32[48,256]{1,0:T(8,128)S(1)}, u32[]{:S(2)}, u32[]{:S(2)}) %collective-permute-start.3) | collective-permute-done | bytes 49184 | tf_op jit(solution)/shard_map/ppermute | solution.py:215
  13.7 0.0 collective-permute-done.4
  13.7 0.0 collective-permute-done.2
  13.7 0.0 copy-start
  13.7 0.0 copy-start.1
  13.7 0.8 %collective-permute-start.5 = (f32[24,256]{1,0:T(8,128)S(1)}, f32[24,256]{1,0:T(8,128)S(1)}, u32[]{:S(2)}, u32[]{:S(2)}) collective-permute-start(f32[24,256]{1,0:T(8,128)S(1)} %get-tuple-element.24), channel_id=1, source_target_pairs={{0,1},{1,0},{2,3},{3,2},{4,5},{5,4},{6,7},{7,6},{8,9},{9,8},{10,11... | collective-permute-start | bytes 73736 | tf_op jit(solution)/shard_map/ppermute | solution.py:215
  14.6 0.8 %collective-permute-done.5 = f32[24,256]{1,0:T(8,128)S(1)} collective-permute-done((f32[24,256]{1,0:T(8,128)S(1)}, f32[24,256]{1,0:T(8,128)S(1)}, u32[]{:S(2)}, u32[]{:S(2)}) %collective-permute-start.5) | collective-permute-done | bytes 24608 | tf_op jit(solution)/shard_map/ppermute | solution.py:215
  15.4 0.0 copy-done
  15.4 0.0 copy-done.1
  15.4 0.3 %solve.1 = (f32[12,256]{1,0:T(8,128)S(1)}, f32[3,4,256]{2,1,0:T(4,128)S(1)}, f32[3,4,256]{2,1,0:T(4,128)S(1)}, f32[3,4,256]{2,1,0:T(4,128)S(1)}) custom-call(f32[1,24,256]{2,1,0:T(8,128)S(1)} %get-tuple-element.25.refs_0_, f32[1,24,256]{2,1,0:T(8,128)S(1)} %bitcast.29, f32[16,1,256]{2,1,0:T(1,128)S(1)} %copy-done, s32[4,1,256]{2,1,0:T(1,128)S(1)} %copy-done.1), custom_call_target="tpu_custom_call" | custom-call | tf_op jit(solution)/shard_map/solve/pallas_call | solution.py:195
  15.7 1.1 %collective-permute-start.6 = (f32[3,4,256]{2,1,0:T(4,128)S(1)}, f32[3,4,256]{2,1,0:T(4,128)S(1)}, u32[]{:S(2)}, u32[]{:S(2)}) collective-permute-start(f32[3,4,256]{2,1,0:T(4,128)S(1)} %get-tuple-element.11), channel_id=1, source_target_pairs={{0,5},{1,4},{2,7},{3,6},{4,1},{5,0},{6,3},{7,2},{8,13},{9,12},{10,... | collective-permute-start | bytes 36872 | tf_op jit(solution)/shard_map/ppermute | solution.py:215
  16.9 0.2 %collective-permute-start.7 = (f32[3,4,256]{2,1,0:T(4,128)S(1)}, f32[3,4,256]{2,1,0:T(4,128)S(1)}, u32[]{:S(2)}, u32[]{:S(2)}) collective-permute-start(f32[3,4,256]{2,1,0:T(4,128)S(1)} %get-tuple-element.12), channel_id=1, source_target_pairs={{0,1},{1,0},{2,3},{3,2},{4,9},{5,8},{6,11},{7,10},{8,5},{9,4},{10,... | collective-permute-start | bytes 36872 | tf_op jit(solution)/shard_map/ppermute | solution.py:215
  17.1 0.3 %collective-permute-start.8 = (f32[3,4,256]{2,1,0:T(4,128)S(1)}, f32[3,4,256]{2,1,0:T(4,128)S(1)}, u32[]{:S(2)}, u32[]{:S(2)}) collective-permute-start(f32[3,4,256]{2,1,0:T(4,128)S(1)} %get-tuple-element.13), channel_id=1, source_target_pairs={{0,1},{1,0},{2,3},{3,2},{4,5},{5,4},{6,7},{7,6},{8,9},{9,8},{10,11... | collective-permute-start | bytes 36872 | tf_op jit(solution)/shard_map/ppermute | solution.py:215
  17.4 1.5 %collective-permute-done.6 = f32[3,4,256]{2,1,0:T(4,128)S(1)} collective-permute-done((f32[3,4,256]{2,1,0:T(4,128)S(1)}, f32[3,4,256]{2,1,0:T(4,128)S(1)}, u32[]{:S(2)}, u32[]{:S(2)}) %collective-permute-start.6) | collective-permute-done | bytes 12320 | tf_op jit(solution)/shard_map/ppermute | solution.py:215
  18.9 0.0 collective-permute-done.7
  18.9 0.0 collective-permute-done.8
  18.9 1.6 %collective-permute-start.10 = (f32[4,256]{1,0:T(4,128)S(1)}, f32[4,256]{1,0:T(4,128)S(1)}, u32[]{:S(2)}, u32[]{:S(2)}) collective-permute-start(f32[4,256]{1,0:T(4,128)S(1)} %get-tuple-element.27), channel_id=1, source_target_pairs={{0,2},{1,3},{2,0},{3,1},{4,6},{5,7},{6,4},{7,5},{8,10},{9,11},{10,... | collective-permute-start | bytes 12296 | tf_op jit(solution)/shard_map/ppermute | solution.py:215
  20.5 0.1 collective-permute-start.9
  20.6 0.6 %copy.8 = f32[12,1,256]{2,1,0:T(1,128)} copy(f32[12,1,256]{2,0,1:T(8,128)S(1)} %bitcast.30) | data formatting | bytes 24576
  21.2 1.4 %collective-permute-done.10 = f32[4,256]{1,0:T(4,128)S(1)} collective-permute-done((f32[4,256]{1,0:T(4,128)S(1)}, f32[4,256]{1,0:T(4,128)S(1)}, u32[]{:S(2)}, u32[]{:S(2)}) %collective-permute-start.10) | collective-permute-done | bytes 4128 | tf_op jit(solution)/shard_map/ppermute | solution.py:215
  22.6 0.0 collective-permute-done.9
  22.6 0.6 %copy.9 = f32[3,1,256]{2,1,0:T(1,128)} copy(f32[3,1,256]{2,0,1:T(4,128)S(1)} %fusion) | data formatting | bytes 6144
  (11 shorter events, 0.1 us)
Async XLA Ops:
  1.9 1.5 %collective-permute-start = (f32[4,24,256]{2,1,0:T(8,128)S(1)}, f32[4,24,256]{2,1,0:T(8,128)S(1)}, u32[]{:S(2)}, u32[]{:S(2)}) collective-permute-start(f32[4,24,256]{2,1,0:T(8,128)S(1)} %get-tuple-element.9), channel_id=1, source_target_pairs={{0,1},{1,0},{2,3},{3,2},{4,5},{5,4},{6,7},{7,6},{8,9},{9,8},{10,11... | collective-permute-start | bytes 294920 | tf_op jit(solution)/shard_map/ppermute | solution.py:215
  3.4 7.6 %collective-permute-start.1 = (f32[48,256]{1,0:T(8,128)S(1)}, f32[48,256]{1,0:T(8,128)S(1)}, u32[]{:S(2)}, u32[]{:S(2)}) collective-permute-start(f32[48,256]{1,0:T(8,128)S(1)} %pad_maximum_fusion), channel_id=1, source_target_pairs={{0,25},{1,28},{2,27},{3,30},{4,29},{5,24},{6,31},{7,26},{8,17},{9,... | collective-permute-start | bytes 147464 | tf_op jit(solution)/shard_map/ppermute | solution.py:215
  8.2 5.5 %collective-permute-start.3 = (f32[48,256]{1,0:T(8,128)S(1)}, f32[48,256]{1,0:T(8,128)S(1)}, u32[]{:S(2)}, u32[]{:S(2)}) collective-permute-start(f32[48,256]{1,0:T(8,128)S(1)} %pad_maximum_fusion.2), channel_id=1, source_target_pairs={{0,17},{1,20},{2,19},{3,22},{4,21},{5,16},{6,23},{7,18},{8,25},{9,... | collective-permute-start | bytes 147464 | tf_op jit(solution)/shard_map/ppermute | solution.py:215
  8.5 5.1 %collective-permute-start.4 = (f32[48,256]{1,0:T(8,128)S(1)}, f32[48,256]{1,0:T(8,128)S(1)}, u32[]{:S(2)}, u32[]{:S(2)}) collective-permute-start(f32[48,256]{1,0:T(8,128)S(1)} %pad_maximum_fusion.3), channel_id=1, source_target_pairs={{0,13},{1,8},{2,15},{3,10},{4,9},{5,12},{6,11},{7,14},{8,5},{9,0},... | collective-permute-start | bytes 147464 | tf_op jit(solution)/shard_map/ppermute | solution.py:215
  9.7 4.0 %collective-permute-start.2 = (f32[48,256]{1,0:T(8,128)S(1)}, f32[48,256]{1,0:T(8,128)S(1)}, u32[]{:S(2)}, u32[]{:S(2)}) collective-permute-start(f32[48,256]{1,0:T(8,128)S(1)} %pad_maximum_fusion.1), channel_id=1, source_target_pairs={{0,5},{1,0},{2,7},{3,2},{4,1},{5,4},{6,3},{7,6},{8,13},{9,8},{10,1... | collective-permute-start | bytes 147464 | tf_op jit(solution)/shard_map/ppermute | solution.py:215
  13.7 1.7 %copy-start = (f32[16,1,256]{2,1,0:T(1,128)S(1)}, f32[16,1,256]{2,1,0:T(1,128)}, u32[]{:S(2)}) copy-start(f32[16,1,256]{2,1,0:T(1,128)} %refs_2_.1) | copy-start | bytes 49156
  13.7 1.7 %copy-start.1 = (s32[4,1,256]{2,1,0:T(1,128)S(1)}, s32[4,1,256]{2,1,0:T(1,128)}, u32[]{:S(2)}) copy-start(s32[4,1,256]{2,1,0:T(1,128)} %refs_3_.3) | copy-start | bytes 12292
  13.7 1.7 %collective-permute-start.5 = (f32[24,256]{1,0:T(8,128)S(1)}, f32[24,256]{1,0:T(8,128)S(1)}, u32[]{:S(2)}, u32[]{:S(2)}) collective-permute-start(f32[24,256]{1,0:T(8,128)S(1)} %get-tuple-element.24), channel_id=1, source_target_pairs={{0,1},{1,0},{2,3},{3,2},{4,5},{5,4},{6,7},{7,6},{8,9},{9,8},{10,11... | collective-permute-start | bytes 73736 | tf_op jit(solution)/shard_map/ppermute | solution.py:215
  15.7 3.2 %collective-permute-start.6 = (f32[3,4,256]{2,1,0:T(4,128)S(1)}, f32[3,4,256]{2,1,0:T(4,128)S(1)}, u32[]{:S(2)}, u32[]{:S(2)}) collective-permute-start(f32[3,4,256]{2,1,0:T(4,128)S(1)} %get-tuple-element.11), channel_id=1, source_target_pairs={{0,5},{1,4},{2,7},{3,6},{4,1},{5,0},{6,3},{7,2},{8,13},{9,12},{10,... | collective-permute-start | bytes 36872 | tf_op jit(solution)/shard_map/ppermute | solution.py:215
  16.9 2.1 %collective-permute-start.7 = (f32[3,4,256]{2,1,0:T(4,128)S(1)}, f32[3,4,256]{2,1,0:T(4,128)S(1)}, u32[]{:S(2)}, u32[]{:S(2)}) collective-permute-start(f32[3,4,256]{2,1,0:T(4,128)S(1)} %get-tuple-element.12), channel_id=1, source_target_pairs={{0,1},{1,0},{2,3},{3,2},{4,9},{5,8},{6,11},{7,10},{8,5},{9,4},{10,... | collective-permute-start | bytes 36872 | tf_op jit(solution)/shard_map/ppermute | solution.py:215
  17.1 1.8 %collective-permute-start.8 = (f32[3,4,256]{2,1,0:T(4,128)S(1)}, f32[3,4,256]{2,1,0:T(4,128)S(1)}, u32[]{:S(2)}, u32[]{:S(2)}) collective-permute-start(f32[3,4,256]{2,1,0:T(4,128)S(1)} %get-tuple-element.13), channel_id=1, source_target_pairs={{0,1},{1,0},{2,3},{3,2},{4,5},{5,4},{6,7},{7,6},{8,9},{9,8},{10,11... | collective-permute-start | bytes 36872 | tf_op jit(solution)/shard_map/ppermute | solution.py:215
  18.9 3.7 %collective-permute-start.10 = (f32[4,256]{1,0:T(4,128)S(1)}, f32[4,256]{1,0:T(4,128)S(1)}, u32[]{:S(2)}, u32[]{:S(2)}) collective-permute-start(f32[4,256]{1,0:T(4,128)S(1)} %get-tuple-element.27), channel_id=1, source_target_pairs={{0,2},{1,3},{2,0},{3,1},{4,6},{5,7},{6,4},{7,5},{8,10},{9,11},{10,... | collective-permute-start | bytes 12296 | tf_op jit(solution)/shard_map/ppermute | solution.py:215
  20.5 2.1 %collective-permute-start.9 = (f32[4,256]{1,0:T(4,128)S(1)}, f32[4,256]{1,0:T(4,128)S(1)}, u32[]{:S(2)}, u32[]{:S(2)}) collective-permute-start(f32[4,256]{1,0:T(4,128)S(1)} %get-tuple-element.28), channel_id=1, source_target_pairs={{0,1},{1,0},{2,3},{3,2},{4,5},{5,4},{6,7},{7,6},{8,9},{9,8},{10,11... | collective-permute-start | bytes 12296 | tf_op jit(solution)/shard_map/ppermute | solution.py:215

commit v7 on v6

--- a/solution.py
+++ b/solution.py
@@ -235,7 +235,7 @@
     if not isinstance(sums, (list, tuple)):
         return [lax.all_to_all(sums, "dom", split_axis=0, concat_axis=0, tiled=True)]
     keep, give = sums
-    other = send(give, stay, near)
+    other = [*send(give[:1], stay, near), *send(give[1:], stay, near)]
     arrived = []
     for j in range(4):
         both = jnp.concatenate([keep[j], other[j]], axis=0)

time: 23.4 us -> 23.3 us (level)
  waiting for transfers between devices: 8.37 us -> 7.81 us
  starting transfers between devices: 11.2 us -> 11.7 us
    ppermute x11 -> x12, waiting for transfers between devices: 8.37 us -> 7.81 us  [send(): return lax.ppermute(array, ('dom', 'slab'), pairs)]
    ppermute x11 -> x12, starting transfers between devices: 11.2 us -> 11.7 us  [send(): return lax.ppermute(array, ('dom', 'slab'), pairs)]
  transfers between devices with their start and end apart: 11 -> 12, of which waited for: 6 -> 6; matrix products, arithmetic and copies ran while one was open for 3% -> 3% of each run, Pallas kernels for 0% -> 0%
where the time goes in v7:
time: 23.3 us; the launch traced here: 23.1 us
  starting transfers between devices  11.7 us (50%)
  waiting for transfers between devices  7.81 us (34%)
  Pallas kernels  1.62 us (7%)
  local copies, waits for them, and re-layouts  1.24 us (5%)
  between operations  0.72 us (3%)
    ppermute x12, starting transfers between devices, send(): return lax.ppermute(array, ('dom', 'slab'), pairs)  11.7 us
    ppermute x12, waiting for transfers between devices, send(): return lax.ppermute(array, ('dom', 'slab'), pairs)  7.81 us
    pallas_call x1, Pallas kernels, partial_sums(): pl.pallas_call(few_doms_kernel if few else many_doms_kernel, grid=(dom_co...  1.31 us
    unnamed x6, local copies, waits for them, and re-layouts  1.21 us
  transfers between devices with their start and end apart: 12, of which 6 were waited for; matrix products, arithmetic and copies ran while one was open for 3% of the time, Pallas kernels for 0%

profile of v7, /device:TPU:0, one launch (start us, length us, event | category | flops | bytes accessed | tf_op | source)
XLA Modules:
  0.0 23.1 jit_solution(14874001077460998054)
XLA Ops:
  0.6 1.3 %partial_sums.1 = (f32[4,24,256]{2,1,0:T(8,128)S(1)}, f32[4,24,256]{2,1,0:T(8,128)S(1)}) custom-call(f32[4,1,1536]{2,1,0:T(1,128)} %refs_0_.1, f32[3,1,1536]{2,1,0:T(1,128)} %refs_1_.1, s32[1,1536]{1,0:T(1,128)} %bitcast.31, s32[1,1536]{1,0:T(1,128)} %refs_3_.2), custom_call_target="tpu_custom_call" | custom-call | tf_op jit(solution)/shard_map/partial_sums/pallas_call | solution.py:112
  2.0 0.5 %collective-permute-start = (f32[1,24,256]{2,1,0:T(8,128)S(1)}, f32[1,24,256]{2,1,0:T(8,128)S(1)}, u32[]{:S(2)}, u32[]{:S(2)}) collective-permute-start(f32[1,24,256]{2,1,0:T(8,128)S(1)} %slice.37), channel_id=1, source_target_pairs={{0,1},{1,0},{2,3},{3,2},{4,5},{5,4},{6,7},{7,6},{8,9},{9,8},{10,11... | collective-permute-start | bytes 73736 | tf_op jit(solution)/shard_map/ppermute | solution.py:215
  2.5 0.1 collective-permute-start.2
  2.6 0.7 %collective-permute-done = f32[1,24,256]{2,1,0:T(8,128)S(1)} collective-permute-done((f32[1,24,256]{2,1,0:T(8,128)S(1)}, f32[1,24,256]{2,1,0:T(8,128)S(1)}, u32[]{:S(2)}, u32[]{:S(2)}) %collective-permute-start) | collective-permute-done | bytes 24608 | tf_op jit(solution)/shard_map/ppermute | solution.py:215
  3.3 4.7 %collective-permute-start.1 = (f32[48,256]{1,0:T(8,128)S(1)}, f32[48,256]{1,0:T(8,128)S(1)}, u32[]{:S(2)}, u32[]{:S(2)}) collective-permute-start(f32[48,256]{1,0:T(8,128)S(1)} %pad_maximum_fusion), channel_id=1, source_target_pairs={{0,25},{1,28},{2,27},{3,30},{4,29},{5,24},{6,31},{7,26},{8,17},{9,... | collective-permute-start | bytes 147464 | tf_op jit(solution)/shard_map/ppermute | solution.py:215
  8.0 0.0 collective-permute-done.2
  8.1 0.4 %collective-permute-start.4 = (f32[48,256]{1,0:T(8,128)S(1)}, f32[48,256]{1,0:T(8,128)S(1)}, u32[]{:S(2)}, u32[]{:S(2)}) collective-permute-start(f32[48,256]{1,0:T(8,128)S(1)} %pad_maximum_fusion.2), channel_id=1, source_target_pairs={{0,17},{1,20},{2,19},{3,22},{4,21},{5,16},{6,23},{7,18},{8,25},{9,... | collective-permute-start | bytes 147464 | tf_op jit(solution)/shard_map/ppermute | solution.py:215
  8.4 1.3 %collective-permute-start.5 = (f32[48,256]{1,0:T(8,128)S(1)}, f32[48,256]{1,0:T(8,128)S(1)}, u32[]{:S(2)}, u32[]{:S(2)}) collective-permute-start(f32[48,256]{1,0:T(8,128)S(1)} %pad_maximum_fusion.3), channel_id=1, source_target_pairs={{0,13},{1,8},{2,15},{3,10},{4,9},{5,12},{6,11},{7,14},{8,5},{9,0},... | collective-permute-start | bytes 147464 | tf_op jit(solution)/shard_map/ppermute | solution.py:215
  9.8 0.5 %collective-permute-start.3 = (f32[48,256]{1,0:T(8,128)S(1)}, f32[48,256]{1,0:T(8,128)S(1)}, u32[]{:S(2)}, u32[]{:S(2)}) collective-permute-start(f32[48,256]{1,0:T(8,128)S(1)} %pad_maximum_fusion.1), channel_id=1, source_target_pairs={{0,5},{1,0},{2,7},{3,2},{4,1},{5,4},{6,3},{7,6},{8,13},{9,8},{10,1... | collective-permute-start | bytes 147464 | tf_op jit(solution)/shard_map/ppermute | solution.py:215
  10.3 0.5 %collective-permute-done.1 = f32[48,256]{1,0:T(8,128)S(1)} collective-permute-done((f32[48,256]{1,0:T(8,128)S(1)}, f32[48,256]{1,0:T(8,128)S(1)}, u32[]{:S(2)}, u32[]{:S(2)}) %collective-permute-start.1) | collective-permute-done | bytes 49184 | tf_op jit(solution)/shard_map/ppermute | solution.py:215
  10.8 2.7 %collective-permute-done.4 = f32[48,256]{1,0:T(8,128)S(1)} collective-permute-done((f32[48,256]{1,0:T(8,128)S(1)}, f32[48,256]{1,0:T(8,128)S(1)}, u32[]{:S(2)}, u32[]{:S(2)}) %collective-permute-start.4) | collective-permute-done | bytes 49184 | tf_op jit(solution)/shard_map/ppermute | solution.py:215
  13.6 0.0 collective-permute-done.5
  13.6 0.0 collective-permute-done.3
  13.6 0.0 copy-start
  13.6 0.0 copy-start.1
  13.6 0.8 %collective-permute-start.6 = (f32[24,256]{1,0:T(8,128)S(1)}, f32[24,256]{1,0:T(8,128)S(1)}, u32[]{:S(2)}, u32[]{:S(2)}) collective-permute-start(f32[24,256]{1,0:T(8,128)S(1)} %get-tuple-element.23), channel_id=1, source_target_pairs={{0,1},{1,0},{2,3},{3,2},{4,5},{5,4},{6,7},{7,6},{8,9},{9,8},{10,11... | collective-permute-start | bytes 73736 | tf_op jit(solution)/shard_map/ppermute | solution.py:215
  14.5 0.8 %collective-permute-done.6 = f32[24,256]{1,0:T(8,128)S(1)} collective-permute-done((f32[24,256]{1,0:T(8,128)S(1)}, f32[24,256]{1,0:T(8,128)S(1)}, u32[]{:S(2)}, u32[]{:S(2)}) %collective-permute-start.6) | collective-permute-done | bytes 24608 | tf_op jit(solution)/shard_map/ppermute | solution.py:215
  15.3 0.0 copy-done
  15.3 0.0 copy-done.1
  15.3 0.3 %solve.1 = (f32[12,256]{1,0:T(8,128)S(1)}, f32[3,4,256]{2,1,0:T(4,128)S(1)}, f32[3,4,256]{2,1,0:T(4,128)S(1)}, f32[3,4,256]{2,1,0:T(4,128)S(1)}) custom-call(f32[1,24,256]{2,1,0:T(8,128)S(1)} %get-tuple-element.24.refs_0_, f32[1,24,256]{2,1,0:T(8,128)S(1)} %bitcast.28, f32[16,1,256]{2,1,0:T(1,128)S(1)} %copy-done, s32[4,1,256]{2,1,0:T(1,128)S(1)} %copy-done.1), custom_call_target="tpu_custom_call" | custom-call | tf_op jit(solution)/shard_map/solve/pallas_call | solution.py:195
  15.6 1.1 %collective-permute-start.7 = (f32[3,4,256]{2,1,0:T(4,128)S(1)}, f32[3,4,256]{2,1,0:T(4,128)S(1)}, u32[]{:S(2)}, u32[]{:S(2)}) collective-permute-start(f32[3,4,256]{2,1,0:T(4,128)S(1)} %get-tuple-element.11), channel_id=1, source_target_pairs={{0,5},{1,4},{2,7},{3,6},{4,1},{5,0},{6,3},{7,2},{8,13},{9,12},{10,... | collective-permute-start | bytes 36872 | tf_op jit(solution)/shard_map/ppermute | solution.py:215
  16.8 0.2 collective-permute-start.8
  17.0 0.3 %collective-permute-start.9 = (f32[3,4,256]{2,1,0:T(4,128)S(1)}, f32[3,4,256]{2,1,0:T(4,128)S(1)}, u32[]{:S(2)}, u32[]{:S(2)}) collective-permute-start(f32[3,4,256]{2,1,0:T(4,128)S(1)} %get-tuple-element.13), channel_id=1, source_target_pairs={{0,1},{1,0},{2,3},{3,2},{4,5},{5,4},{6,7},{7,6},{8,9},{9,8},{10,11... | collective-permute-start | bytes 36872 | tf_op jit(solution)/shard_map/ppermute | solution.py:215
  17.3 1.5 %collective-permute-done.7 = f32[3,4,256]{2,1,0:T(4,128)S(1)} collective-permute-done((f32[3,4,256]{2,1,0:T(4,128)S(1)}, f32[3,4,256]{2,1,0:T(4,128)S(1)}, u32[]{:S(2)}, u32[]{:S(2)}) %collective-permute-start.7) | collective-permute-done | bytes 12320 | tf_op jit(solution)/shard_map/ppermute | solution.py:215
  18.8 0.0 collective-permute-done.8
  18.8 0.0 collective-permute-done.9
  18.9 1.6 %collective-permute-start.11 = (f32[4,256]{1,0:T(4,128)S(1)}, f32[4,256]{1,0:T(4,128)S(1)}, u32[]{:S(2)}, u32[]{:S(2)}) collective-permute-start(f32[4,256]{1,0:T(4,128)S(1)} %get-tuple-element.26), channel_id=1, source_target_pairs={{0,2},{1,3},{2,0},{3,1},{4,6},{5,7},{6,4},{7,5},{8,10},{9,11},{10,... | collective-permute-start | bytes 12296 | tf_op jit(solution)/shard_map/ppermute | solution.py:215
  20.4 0.1 collective-permute-start.10
  20.5 0.6 %copy.8 = f32[12,1,256]{2,1,0:T(1,128)} copy(f32[12,1,256]{2,0,1:T(8,128)S(1)} %bitcast.29) | data formatting | bytes 24576
  21.1 1.4 %collective-permute-done.11 = f32[4,256]{1,0:T(4,128)S(1)} collective-permute-done((f32[4,256]{1,0:T(4,128)S(1)}, f32[4,256]{1,0:T(4,128)S(1)}, u32[]{:S(2)}, u32[]{:S(2)}) %collective-permute-start.11) | collective-permute-done | bytes 4128 | tf_op jit(solution)/shard_map/ppermute | solution.py:215
  22.5 0.0 collective-permute-done.10
  22.5 0.6 %copy.9 = f32[3,1,256]{2,1,0:T(1,128)} copy(f32[3,1,256]{2,0,1:T(4,128)S(1)} %fusion) | data formatting | bytes 6144
  (13 shorter events, 0.1 us)
Async XLA Ops:
  2.0 1.4 %collective-permute-start = (f32[1,24,256]{2,1,0:T(8,128)S(1)}, f32[1,24,256]{2,1,0:T(8,128)S(1)}, u32[]{:S(2)}, u32[]{:S(2)}) collective-permute-start(f32[1,24,256]{2,1,0:T(8,128)S(1)} %slice.37), channel_id=1, source_target_pairs={{0,1},{1,0},{2,3},{3,2},{4,5},{5,4},{6,7},{7,6},{8,9},{9,8},{10,11... | collective-permute-start | bytes 73736 | tf_op jit(solution)/shard_map/ppermute | solution.py:215
  2.5 5.6 %collective-permute-start.2 = (f32[3,24,256]{2,1,0:T(8,128)S(1)}, f32[3,24,256]{2,1,0:T(8,128)S(1)}, u32[]{:S(2)}, u32[]{:S(2)}) collective-permute-start(f32[3,24,256]{2,1,0:T(8,128)S(1)} %slice.39), channel_id=1, source_target_pairs={{0,1},{1,0},{2,3},{3,2},{4,5},{5,4},{6,7},{7,6},{8,9},{9,8},{10,11... | collective-permute-start | bytes 221192 | tf_op jit(solution)/shard_map/ppermute | solution.py:215
  3.3 7.5 %collective-permute-start.1 = (f32[48,256]{1,0:T(8,128)S(1)}, f32[48,256]{1,0:T(8,128)S(1)}, u32[]{:S(2)}, u32[]{:S(2)}) collective-permute-start(f32[48,256]{1,0:T(8,128)S(1)} %pad_maximum_fusion), channel_id=1, source_target_pairs={{0,25},{1,28},{2,27},{3,30},{4,29},{5,24},{6,31},{7,26},{8,17},{9,... | collective-permute-start | bytes 147464 | tf_op jit(solution)/shard_map/ppermute | solution.py:215
  8.1 5.5 %collective-permute-start.4 = (f32[48,256]{1,0:T(8,128)S(1)}, f32[48,256]{1,0:T(8,128)S(1)}, u32[]{:S(2)}, u32[]{:S(2)}) collective-permute-start(f32[48,256]{1,0:T(8,128)S(1)} %pad_maximum_fusion.2), channel_id=1, source_target_pairs={{0,17},{1,20},{2,19},{3,22},{4,21},{5,16},{6,23},{7,18},{8,25},{9,... | collective-permute-start | bytes 147464 | tf_op jit(solution)/shard_map/ppermute | solution.py:215
  8.4 5.1 %collective-permute-start.5 = (f32[48,256]{1,0:T(8,128)S(1)}, f32[48,256]{1,0:T(8,128)S(1)}, u32[]{:S(2)}, u32[]{:S(2)}) collective-permute-start(f32[48,256]{1,0:T(8,128)S(1)} %pad_maximum_fusion.3), channel_id=1, source_target_pairs={{0,13},{1,8},{2,15},{3,10},{4,9},{5,12},{6,11},{7,14},{8,5},{9,0},... | collective-permute-start | bytes 147464 | tf_op jit(solution)/shard_map/ppermute | solution.py:215
  9.8 3.8 %collective-permute-start.3 = (f32[48,256]{1,0:T(8,128)S(1)}, f32[48,256]{1,0:T(8,128)S(1)}, u32[]{:S(2)}, u32[]{:S(2)}) collective-permute-start(f32[48,256]{1,0:T(8,128)S(1)} %pad_maximum_fusion.1), channel_id=1, source_target_pairs={{0,5},{1,0},{2,7},{3,2},{4,1},{5,4},{6,3},{7,6},{8,13},{9,8},{10,1... | collective-permute-start | bytes 147464 | tf_op jit(solution)/shard_map/ppermute | solution.py:215
  13.6 1.7 %copy-start = (f32[16,1,256]{2,1,0:T(1,128)S(1)}, f32[16,1,256]{2,1,0:T(1,128)}, u32[]{:S(2)}) copy-start(f32[16,1,256]{2,1,0:T(1,128)} %refs_2_.1) | copy-start | bytes 49156
  13.6 1.7 %copy-start.1 = (s32[4,1,256]{2,1,0:T(1,128)S(1)}, s32[4,1,256]{2,1,0:T(1,128)}, u32[]{:S(2)}) copy-start(s32[4,1,256]{2,1,0:T(1,128)} %refs_3_.3) | copy-start | bytes 12292
  13.6 1.7 %collective-permute-start.6 = (f32[24,256]{1,0:T(8,128)S(1)}, f32[24,256]{1,0:T(8,128)S(1)}, u32[]{:S(2)}, u32[]{:S(2)}) collective-permute-start(f32[24,256]{1,0:T(8,128)S(1)} %get-tuple-element.23), channel_id=1, source_target_pairs={{0,1},{1,0},{2,3},{3,2},{4,5},{5,4},{6,7},{7,6},{8,9},{9,8},{10,11... | collective-permute-start | bytes 73736 | tf_op jit(solution)/shard_map/ppermute | solution.py:215
  15.6 3.2 %collective-permute-start.7 = (f32[3,4,256]{2,1,0:T(4,128)S(1)}, f32[3,4,256]{2,1,0:T(4,128)S(1)}, u32[]{:S(2)}, u32[]{:S(2)}) collective-permute-start(f32[3,4,256]{2,1,0:T(4,128)S(1)} %get-tuple-element.11), channel_id=1, source_target_pairs={{0,5},{1,4},{2,7},{3,6},{4,1},{5,0},{6,3},{7,2},{8,13},{9,12},{10,... | collective-permute-start | bytes 36872 | tf_op jit(solution)/shard_map/ppermute | solution.py:215
  16.8 2.0 %collective-permute-start.8 = (f32[3,4,256]{2,1,0:T(4,128)S(1)}, f32[3,4,256]{2,1,0:T(4,128)S(1)}, u32[]{:S(2)}, u32[]{:S(2)}) collective-permute-start(f32[3,4,256]{2,1,0:T(4,128)S(1)} %get-tuple-element.12), channel_id=1, source_target_pairs={{0,1},{1,0},{2,3},{3,2},{4,9},{5,8},{6,11},{7,10},{8,5},{9,4},{10,... | collective-permute-start | bytes 36872 | tf_op jit(solution)/shard_map/ppermute | solution.py:215
  17.0 1.8 %collective-permute-start.9 = (f32[3,4,256]{2,1,0:T(4,128)S(1)}, f32[3,4,256]{2,1,0:T(4,128)S(1)}, u32[]{:S(2)}, u32[]{:S(2)}) collective-permute-start(f32[3,4,256]{2,1,0:T(4,128)S(1)} %get-tuple-element.13), channel_id=1, source_target_pairs={{0,1},{1,0},{2,3},{3,2},{4,5},{5,4},{6,7},{7,6},{8,9},{9,8},{10,11... | collective-permute-start | bytes 36872 | tf_op jit(solution)/shard_map/ppermute | solution.py:215
  18.9 3.7 %collective-permute-start.11 = (f32[4,256]{1,0:T(4,128)S(1)}, f32[4,256]{1,0:T(4,128)S(1)}, u32[]{:S(2)}, u32[]{:S(2)}) collective-permute-start(f32[4,256]{1,0:T(4,128)S(1)} %get-tuple-element.26), channel_id=1, source_target_pairs={{0,2},{1,3},{2,0},{3,1},{4,6},{5,7},{6,4},{7,5},{8,10},{9,11},{10,... | collective-permute-start | bytes 12296 | tf_op jit(solution)/shard_map/ppermute | solution.py:215
  20.4 2.1 %collective-permute-start.10 = (f32[4,256]{1,0:T(4,128)S(1)}, f32[4,256]{1,0:T(4,128)S(1)}, u32[]{:S(2)}, u32[]{:S(2)}) collective-permute-start(f32[4,256]{1,0:T(4,128)S(1)} %get-tuple-element.27), channel_id=1, source_target_pairs={{0,1},{1,0},{2,3},{3,2},{4,5},{5,4},{6,7},{7,6},{8,9},{9,8},{10,11... | collective-permute-start | bytes 12296 | tf_op jit(solution)/shard_map/ppermute | solution.py:215
